TPU v7x, 32 devices: a whole 2x2x4 slice. The times are simulated.
32 devices in a mesh: img: 16 (over z, x, core), fou: 2 (over y).
Axes of the slice: x: 2, y: 2, z: 4, core: 2. Of those that a mesh axis runs over, the one named last changes fastest.
Arguments:
- sky_estimate: float32 [4, 2048, 2048], P(None, 'img', 'fou'), may hold values from 0 to 2
- dual_coeffs: bfloat16 [4, 9, 2048, 2048], P(None, None, 'img', 'fou'), may hold values from -2 to 2
- dirty_image: float32 [4, 2048, 2048], P(None, 'img', 'fou'), may hold values from -4 to 4
- filters: float32 [8, 17], replicated, may hold values from -1.5 to 1.5
- thresholds: float32 [9], replicated, may hold values from 0.2 to 1.2
- facet_rows: int32 [16], P('img'), may hold values from 32 to 128, as said below
- tile_slots: int32 [4, 32, 6], P(None, 'img'), may hold values from 0 to 31, as said below
- tile_count: int32 [4, 32], P(None, 'img'), may hold values from 1 to 6, as said below
- gram_tiles: bfloat16 [4, 32, 6, 64, 64], P(None, 'img'), may hold values from -4 to 4
Outputs:
- image_next: float32 [4, 2048, 2048], P(None, 'img', 'fou')
- dual_next: bfloat16 [4, 9, 2048, 2048], P(None, None, 'img', 'fou')
Inputs may be any that keep to these rules, and one draw needn't show every extreme that they name: `facet_rows`: facet f covers image rows f * 128 to (f + 1) * 128 - 1; some facet is full. `tile_slots`: the 6 entries of one channel and v-tile are distinct. `tile_count`: slots at or beyond the count hold no tile; in each channel some v-tile uses all 6 slots.
All inputs are finite; a program needn't handle non-finite values.
Results may differ from a plain program's by a relative error of at most 0.005.
Values may be sent and summed in bfloat16 or wider, within the bound.
A program may use at most 192 MiB of HBM per device.

v0:
```python
import functools
import math

import jax
import jax.numpy as jnp
import numpy as np
from jax import lax
from jax.experimental import pallas as pl
from jax.experimental.pallas import tpu as pltpu
from jax.sharding import PartitionSpec as P

STEP_PRIMAL = 0.5
STEP_DUAL = 0.5
LANES = 128
BF16 = jnp.bfloat16
F32 = jnp.float32


def dot(a, b, dims=((1,), (0,)), **kw):
    return lax.dot_general(a, b, (dims, ((), ())), preferred_element_type=F32, **kw)


def flip_halves(x):
    half = x.shape[-1] // 2
    return jnp.concatenate([x[:, half:], x[:, :half]], axis=1)


def half_sign(rows, lanes, dtype=F32):
    lane = lax.broadcasted_iota(jnp.int32, (rows, lanes), 1)
    return jnp.where(lane < lanes // 2, 1.0, -1.0).astype(dtype)


def tables(line, block):
    small = np.arange(block)[:, None] * np.arange(line)[None, :] % line
    angle = small * (2.0 * math.pi / line)
    by_row = np.concatenate([np.cos(angle), np.sin(angle)], axis=0).astype(np.float32)
    period = line // block
    turn = np.arange(period)[:, None] * np.arange(period)[None, :] % period
    turn = turn * (2.0 * math.pi / period)
    return by_row, np.cos(turn).astype(np.float32), np.sin(turn).astype(np.float32)


def turned(base, other, cos_tile, sin_tile):
    rows, lanes = base.shape
    period = cos_tile.shape[0]
    base = base.reshape(rows // period, period, lanes)
    other = other.reshape(rows // period, period, lanes)
    out = base * cos_tile[None] + other * sin_tile[None]
    return out.reshape(rows, lanes).astype(BF16)


def forward_kernel(x_ref, et_ref, es_ref, pc_ref, ps_ref, o_ref):
    both = [turned(et_ref[...], es_ref[...], pc_ref[i], ps_ref[i]) for i in range(2)]
    lanes = et_ref.shape[1]
    out = dot(x_ref[...], jnp.concatenate(both, axis=1))
    sign = half_sign(1, lanes)
    for i in range(2):
        o_ref[i] = (out[:, i * lanes : (i + 1) * lanes] * sign).astype(BF16)


def forward(x, et, es, pc, ps):
    rows, line = x.shape
    tiles, period, lanes = pc.shape
    whole = pl.BlockSpec((line, lanes), lambda i: (0, 0))
    turn = pl.BlockSpec((2, period, lanes), lambda i: (i, 0, 0))
    return pl.pallas_call(
        forward_kernel,
        grid=(tiles // 2,),
        in_specs=[pl.BlockSpec((rows, line), lambda i: (0, 0)), whole, whole, turn, turn],
        out_specs=pl.BlockSpec((2, rows, lanes), lambda i: (i, 0, 0)),
        out_shape=jax.ShapeDtypeStruct((tiles, rows, lanes), BF16),
        name="forward",
    )(x, et, es, pc, ps)


def backward_kernel(scale, y_ref, et_ref, es_ref, pc_ref, ps_ref, o_ref, all_y, table):
    tiles, rows, lanes = y_ref.shape

    @pl.when(pl.program_id(0) == 0)
    def _():
        sign = half_sign(1, lanes)
        for q in range(tiles):
            all_y[:, q * lanes : (q + 1) * lanes] = (y_ref[q].astype(F32) * sign).astype(BF16)

    for q in range(tiles):
        table[:, q * lanes : (q + 1) * lanes] = turned(
            et_ref[...], es_ref[...], pc_ref[q], ps_ref[q]
        )
    out = dot(all_y[...], table[...], ((1,), (1,)))
    o_ref[...] = (out * scale).astype(BF16)


def backward(y, et, es, pc, ps, scale):
    tiles, rows, lanes = y.shape
    line = et.shape[0]
    part = min(256, line)
    chunk = pl.BlockSpec((part, lanes), lambda i: (i, 0))
    fixed = pl.BlockSpec(pc.shape, lambda i: (0, 0, 0))
    return pl.pallas_call(
        functools.partial(backward_kernel, scale),
        grid=(line // part,),
        in_specs=[pl.BlockSpec((tiles, rows, lanes), lambda i: (0, 0, 0)), chunk, chunk, fixed, fixed],
        out_specs=pl.BlockSpec((rows, part), lambda i: (0, i)),
        out_shape=jax.ShapeDtypeStruct((rows, line), BF16),
        scratch_shapes=[
            pltpu.VMEM((rows, tiles * lanes), BF16),
            pltpu.VMEM((part, tiles * lanes), BF16),
        ],
        name="backward",
    )(y, et, es, pc, ps)


def gram_kernel(slots_ref, x_ref, g_ref, e_ref, et_ref, es_ref, rc_ref, rs_ref, pc_ref, ps_ref,
                o_ref, table, table_t):
    c = pl.program_id(0)
    parts, _, rows, lanes = x_ref.shape
    wide, line = e_ref.shape
    block = wide // 2
    slots = g_ref.shape[1]
    x = x_ref[:, 0].reshape(parts * rows, lanes)
    top, low = e_ref[:block], e_ref[block:]
    for k in range(slots):
        t = slots_ref[c, k]
        cos_row = rc_ref[pl.ds(t, 1), :]
        sin_row = rs_ref[pl.ds(t, 1), :]
        table[k * wide : k * wide + block] = (top * cos_row - low * sin_row).astype(BF16)
        table[k * wide + block : (k + 1) * wide] = (low * cos_row + top * sin_row).astype(BF16)
        table_t[:, k * wide : (k + 1) * wide] = turned(
            et_ref[...], es_ref[...], pc_ref[t], ps_ref[t]
        )
    first = dot(table[...], x)
    sign = half_sign(1, lanes)
    stack = []
    for k in range(slots):
        cos_part = first[k * wide : k * wide + block]
        sin_part = first[k * wide + block : (k + 1) * wide]
        spec = cos_part + flip_halves(sin_part) * sign
        out = dot(g_ref[0, k], spec, precision=lax.Precision.HIGHEST)
        stack += [out, flip_halves(out) * -sign]
    stack = jnp.concatenate(stack, axis=0)
    high = stack.astype(BF16)
    low_part = (stack - high.astype(F32)).astype(BF16)
    back = dot(table_t[...], high) + dot(table_t[...], low_part)
    o_ref[:, 0] = back.astype(BF16).reshape(parts, rows, lanes)


def gram(x, slots, g_t, e, et, es, rc, rs, pc, ps):
    parts, channels, rows, lanes = x.shape
    wide, line = e.shape
    count = g_t.shape[1]

    def fixed(a):
        return pl.BlockSpec(a.shape, lambda i, s: (0,) * a.ndim)

    data = pl.BlockSpec((parts, 1, rows, lanes), lambda i, s: (0, i, 0, 0))
    return pl.pallas_call(
        gram_kernel,
        grid_spec=pltpu.PrefetchScalarGridSpec(
            num_scalar_prefetch=1,
            grid=(channels,),
            in_specs=[
                data,
                pl.BlockSpec((1,) + g_t.shape[1:], lambda i, s: (i, 0, 0, 0)),
                fixed(e), fixed(et), fixed(es), fixed(rc), fixed(rs), fixed(pc), fixed(ps),
            ],
            out_specs=data,
            scratch_shapes=[
                pltpu.VMEM((count * wide, line), BF16),
                pltpu.VMEM((line, count * wide), BF16),
            ],
        ),
        out_shape=jax.ShapeDtypeStruct(x.shape, BF16),
        name="gram",
    )(slots, x, g_t, e, et, es, rc, rs, pc, ps)


def synthesis_kernel(d_ref, col_ref, row_ref, o_ref, across):
    _, frames, rows, cols = d_ref.shape
    parts = cols // LANES
    for f in range(frames):
        zero = jnp.zeros((rows, LANES), BF16)
        windows = [jnp.concatenate([zero, d_ref[0, f, :, :LANES]], axis=1)]
        for j in range(1, parts):
            windows.append(d_ref[0, f, :, (j - 1) * LANES : (j + 1) * LANES])
        windows.append(jnp.concatenate([d_ref[0, f, :, cols - LANES :], zero], axis=1))
        out = dot(jnp.concatenate(windows, axis=0), col_ref[f]).astype(BF16)
        for j in range(parts + 1):
            across[f * rows : (f + 1) * rows, j * LANES : (j + 1) * LANES] = out[
                j * rows : (j + 1) * rows
            ]
    o_ref[0] = dot(row_ref[...], across[...])


def synthesize(dual, col_band, row_band):
    channels, frames, rows, cols = dual.shape
    wide = cols + LANES
    tall = row_band.shape[0]
    return pl.pallas_call(
        synthesis_kernel,
        grid=(channels,),
        in_specs=[
            pl.BlockSpec((1, frames, rows, cols), lambda c: (c, 0, 0, 0)),
            pl.BlockSpec(col_band.shape, lambda c: (0, 0, 0)),
            pl.BlockSpec(row_band.shape, lambda c: (0, 0)),
        ],
        out_specs=pl.BlockSpec((1, tall, wide), lambda c: (c, 0, 0)),
        out_shape=jax.ShapeDtypeStruct((channels, tall, wide), F32),
        scratch_shapes=[pltpu.VMEM((frames * rows, wide), BF16)],
        cost_estimate=pl.CostEstimate(
            flops=channels * frames * rows * wide * 800, bytes_accessed=dual.size * 2, transcendentals=0
        ),
        name="synthesis",
    )(dual, col_band, row_band)


def analysis_kernel(bound_ref, p_ref, d_ref, col_ref, row_ref, o_ref, cand):
    channels, _, rows, cols = d_ref.shape
    tall = p_ref.shape[1]
    parts = cols // LANES
    bound = bound_ref[pl.program_id(0)]
    total = None
    for c in range(channels):
        windows = [p_ref[c, :, j * LANES : (j + 2) * LANES] for j in range(parts)]
        out = dot(jnp.concatenate(windows, axis=0), col_ref[0]).astype(BF16)
        across = jnp.concatenate([out[j * tall : (j + 1) * tall] for j in range(parts)], axis=1)
        new = d_ref[c, 0].astype(F32) + STEP_DUAL * dot(row_ref[0], across)
        cand[c] = new
        total = new * new if total is None else total + new * new
    scale = bound / jnp.maximum(jnp.sqrt(total), bound)
    for c in range(channels):
        o_ref[c, 0] = (cand[c] * scale).astype(BF16)


def analyse(probe, dual, col_band, row_band, bounds):
    channels, frames, rows, cols = dual.shape
    block = pl.BlockSpec((channels, 1, rows, cols), lambda f: (0, f, 0, 0))
    return pl.pallas_call(
        analysis_kernel,
        grid=(frames,),
        in_specs=[
            pl.BlockSpec(memory_space=pltpu.SMEM),
            pl.BlockSpec(probe.shape, lambda f: (0, 0, 0)),
            block,
            pl.BlockSpec((1,) + col_band.shape[1:], lambda f: (f, 0, 0)),
            pl.BlockSpec((1,) + row_band.shape[1:], lambda f: (f, 0, 0)),
        ],
        out_specs=block,
        out_shape=jax.ShapeDtypeStruct(dual.shape, BF16),
        scratch_shapes=[pltpu.VMEM((channels, rows, cols), F32)],
        name="analysis",
    )(bounds, probe, dual, col_band, row_band)


def banded(taps, offset):
    count = taps.shape[1]
    out = jnp.zeros((taps.shape[0],) + offset.shape, F32)
    for tap in range(count):
        hit = jnp.asarray(offset) == tap
        out = jnp.where(hit[None], taps[:, tap][:, None, None], out)
    return out.astype(BF16)


def shift_up(x, axis):
    count = lax.axis_size(axis)
    return lax.ppermute(x, axis, [(i, i + 1) for i in range(count - 1)])


def shift_down(x, axis):
    count = lax.axis_size(axis)
    return lax.ppermute(x, axis, [(i + 1, i) for i in range(count - 1)])


def body(sky, dual, dirty, filters, thresholds, facet_rows, tile_slots, tile_count, gram_tiles):
    channels, rows, cols = sky.shape
    taps_len = filters.shape[1]
    radius = (taps_len - 1) // 2
    fou = lax.axis_size("fou")
    img = lax.axis_size("img")
    devices = img * fou
    line = cols * fou
    block = gram_tiles.shape[-1]
    slots = gram_tiles.shape[2]
    tiles = line // block
    slab = rows // fou
    width = line // devices
    axes = ("img", "fou")

    by_row, cos_turn, sin_turn = tables(line, block)
    e = jnp.asarray(by_row)
    et = jnp.asarray(np.ascontiguousarray(by_row.T))
    es = jnp.concatenate([-et[:, block:], et[:, :block]], axis=1)
    lanes = 2 * block
    pc = jnp.broadcast_to(jnp.asarray(cos_turn)[:, :, None], (tiles, tiles, lanes))
    ps = jnp.broadcast_to(jnp.asarray(sin_turn)[:, :, None], (tiles, tiles, lanes))
    rc = jnp.tile(jnp.asarray(cos_turn), (1, line // tiles))
    rs = jnp.tile(jnp.asarray(sin_turn), (1, line // tiles))

    lines = lax.all_to_all(sky.astype(BF16), "fou", split_axis=1, concat_axis=2, tiled=True)
    spread = forward(lines.reshape(channels * slab, line), et, es, pc, ps)
    spread = spread.reshape(tiles, channels, slab, lanes)
    per = block // width
    if per > 1:
        spread = spread.reshape(tiles, channels, slab, 2, per, width)
        spread = spread.transpose(0, 4, 1, 2, 3, 5).reshape(devices, channels, slab, 2 * width)
    moved = lax.all_to_all(spread, axes, split_axis=0, concat_axis=0, tiled=True)

    identity = (jnp.arange(taps_len) == radius).astype(F32)
    taps = jnp.concatenate([identity[None], filters], axis=0)
    frames = taps.shape[0]
    tall = rows + 2 * radius
    near = np.arange(2 * LANES)[:, None]
    synth_col = banded(taps, np.arange(LANES)[None, :] + LANES - near)
    synth_row = banded(taps, np.arange(tall)[:, None] - np.arange(rows)[None, :])
    synth_row = synth_row.transpose(1, 0, 2).reshape(tall, frames * rows)
    ana_col = banded(taps, near - np.arange(LANES)[None, :])
    ana_row = banded(taps, np.arange(tall)[None, :] - np.arange(rows)[:, None])
    ext = synthesize(dual, synth_col, synth_row)
    mid = ext[:, :, radius : radius + cols]
    from_left = shift_up(ext[:, :, radius + cols : cols + 2 * radius], "fou")
    from_right = shift_down(ext[:, :, :radius], "fou")
    rest = cols - radius
    mid = mid + jnp.pad(from_left, ((0, 0), (0, 0), (0, rest))) + jnp.pad(
        from_right, ((0, 0), (0, 0), (rest, 0))
    )
    from_above = shift_up(mid[:, radius + rows :], "img")
    from_below = shift_down(mid[:, :radius], "img")
    rest = rows - radius
    synthesis = (
        mid[:, radius : radius + rows]
        + jnp.pad(from_above, ((0, 0), (0, rest), (0, 0)))
        + jnp.pad(from_below, ((0, 0), (rest, 0), (0, 0)))
    )

    which = lax.axis_index("fou") * width // block
    tile_g = lax.dynamic_index_in_dim(gram_tiles, which, 1, keepdims=False).astype(F32)
    chosen = lax.dynamic_index_in_dim(tile_slots, which, 1, keepdims=False)
    used = lax.dynamic_index_in_dim(tile_count, which, 1, keepdims=False)
    in_use = jnp.arange(slots)[None, :] < used[:, None]
    tile_g = jnp.where(in_use[:, :, None, None], jnp.swapaxes(tile_g, -1, -2), 0.0)

    if slab % 16:
        x = moved.transpose(1, 0, 2, 3).reshape(1, channels, line, 2 * width)
    else:
        x = moved
    y = gram(x, chosen, tile_g, e, et, es, rc, rs, pc, ps)
    if slab % 16:
        y = y.reshape(channels, devices, slab, 2 * width).transpose(1, 0, 2, 3)
    back = lax.all_to_all(y, axes, split_axis=0, concat_axis=0, tiled=True)
    if per > 1:
        back = back.reshape(tiles, per, channels, slab, 2, width).transpose(0, 2, 3, 4, 1, 5)
    back = back.reshape(tiles, channels * slab, lanes)
    final = backward(back, et, es, pc, ps, 1.0 / float(line * line))
    gram_image = lax.all_to_all(
        final.reshape(channels, slab, line), "fou", split_axis=2, concat_axis=1, tiled=True
    ).astype(F32)

    live_rows = (jnp.arange(rows, dtype=jnp.int32) < facet_rows[0]).astype(F32)
    image_next = (
        jnp.maximum(sky - STEP_PRIMAL * (gram_image - dirty + synthesis), 0.0)
        * live_rows[None, :, None]
    )
    probe = (2.0 * image_next - sky).astype(BF16)
    probe = jnp.concatenate(
        [shift_up(probe[:, rows - radius :], "img"), probe, shift_down(probe[:, :radius], "img")],
        axis=1,
    )
    probe = jnp.concatenate(
        [
            shift_up(probe[:, :, cols - radius :], "fou"),
            probe,
            shift_down(probe[:, :, :radius], "fou"),
            jnp.zeros((channels, tall, LANES - 2 * radius), BF16),
        ],
        axis=2,
    )
    dual_next = analyse(probe, dual, ana_col, ana_row, thresholds)
    return (image_next, dual_next)


def solution(mesh):
    in_specs = (
        P(None, "img", "fou"),
        P(None, None, "img", "fou"),
        P(None, "img", "fou"),
        P(),
        P(),
        P("img"),
        P(None, "img", None),
        P(None, "img"),
        P(None, "img", None, None, None),
    )
    out_specs = (P(None, "img", "fou"), P(None, None, "img", "fou"))
    return jax.shard_map(body, mesh=mesh, in_specs=in_specs, out_specs=out_specs, check_vma=False)
```

profile of v0, /device:TPU:0, one launch (start us, length us, event | category | flops | bytes accessed | tf_op | source)
XLA Modules:
  0.0 268.5 jit_solution(4252570966602152627)
XLA Ops:
  0.6 3.0 %copy.73 = bf16[4,128,1024]{2,0,1:T(4,128)(2,1)S(1)} copy(f32[4,128,1024]{2,1,0:T(8,128)} %param.17) | data formatting | bytes 3145728 | tf_op args[0]
  3.7 17.7 %all_to_all.34 = bf16[4,128,1024]{2,0,1:T(4,128)(2,1)S(1)} all-to-all(bf16[4,128,1024]{2,0,1:T(4,128)(2,1)S(1)} %copy.73), channel_id=1, replica_groups=mesh['img'=16,'fou'=2] {'fou'}, dimensions={1} | all-to-all | bytes 2097152 | tf_op jit(solution)/shard_map/all_to_all | solution.py:298
  25.7 12.9 %forward.1 = bf16[32,256,128]{2,1,0:T(8,128)(2,1)} custom-call(bf16[256,2048]{1,0:T(8,128)(2,1)} %bitcast.153, f32[2048,128]{1,0:T(8,128)} %constant.59.clone.et_ref, f32[2048,128]{1,0:T(8,128)} %constant.72.es_ref, f32[32,32,128]{2,1,0:T(8,128)} %broadcast_in_dim.906.pc_ref, f32[32,32,128]{2,1,0:T(8,128)} %broadcast_in_dim.907.ps_ref), custom_call_target="tpu_custom_call" | custom-call | tf_op jit(solution)/shard_map/forward/pallas_call | solution.py:66
  38.6 5.0 %all-to-all-start.1 = ((bf16[32,4,64,128]{3,2,1,0:T(8,128)(2,1)}), bf16[32,4,64,128]{3,2,1,0:T(8,128)(2,1)S(1)}, u32[]{:S(2)}, u32[]{:S(2)}) async-start(bf16[32,4,64,128]{3,2,1,0:T(8,128)(2,1)} %bitcast.146), calls=%async_computation.1 | async-start | bytes 4194304 | tf_op jit(solution)/shard_map/all_to_all | solution.py:305
  45.0 2.5 tile.9.rc_ref
  48.5 2.4 tile.21.rs_ref
  52.6 39.7 %all-to-all-done.1.x_ref = bf16[32,4,64,128]{3,2,1,0:T(8,128)(2,1)S(1)} async-done(((bf16[32,4,64,128]{3,2,1,0:T(8,128)(2,1)}), bf16[32,4,64,128]{3,2,1,0:T(8,128)(2,1)S(1)}, u32[]{:S(2)}, u32[]{:S(2)}) %all-to-all-start.1) | async-done | bytes 2097184 | tf_op jit(solution)/shard_map/all_to_all | solution.py:305
  93.7 22.5 %gram.1 = bf16[32,4,64,128]{3,2,1,0:T(8,128)(2,1)} custom-call(s32[4,6]{1,0:T(4,128)} %bitcast.205, bf16[32,4,64,128]{3,2,1,0:T(8,128)(2,1)} %copy-done.4, f32[4,6,64,64]{3,2,1,0:T(8,128)} %fusion.7.g_ref, f32[128,2048]{1,0:T(8,128)} %constant.58.clone.e_ref, f32[2048,128]{1,0:T(8,128)} %constant.59.clone.et_ref, f32[2048,128]{1,0:T(8,128)} %constant.72.es_ref, ...), custom_call_target="tpu_custom_call" | custom-call | tf_op jit(solution)/shard_map/gram/pallas_call | solution.py:156
  116.4 3.8 %all-to-all-start.2 = ((bf16[32,4,64,128]{3,2,1,0:T(8,128)(2,1)}), bf16[32,4,64,128]{3,2,1,0:T(8,128)(2,1)S(1)}, u32[]{:S(2)}, u32[]{:S(2)}) async-start(bf16[32,4,64,128]{3,2,1,0:T(8,128)(2,1)} %gram.1), calls=%async_computation.2 | async-start | bytes 4194304 | tf_op jit(solution)/shard_map/all_to_all | solution.py:348
  121.9 2.9 %select_convert_fusion.2.col_ref = bf16[9,256,128]{2,1,0:T(8,128)(2,1)} fusion(bf16[9]{0:T(256)(128)(2,1)S(1)} %get-tuple-element.17, bf16[9]{0:T(256)(128)(2,1)S(1)} %get-tuple-element.18, bf16[9]{0:T(256)(128)(2,1)S(1)} %get-tuple-element.16, bf16[9]{0:T(256)(128)(2,1)S(1)} %get-tuple-element.15, bf16[9]{0:T(256)(128)(2,1)S(1)} %get-tuple-element.14, ...), kind=kLoop, calls=%fused_computation.15 | loop fusion | flops 5013504 | bytes 1147186 | tf_op jit(solution)/shard_map/convert_element_type | solution.py:260
  126.7 2.3 select_convert_fusion.3.row_ref
  129.0 11.1 %synthesis.1 = f32[4,144,1152]{2,1,0:T(8,128)} custom-call(bf16[4,9,128,1024]{3,2,1,0:T(8,128)(2,1)} %d_ref.3, bf16[9,256,128]{2,1,0:T(8,128)(2,1)} %select_convert_fusion.2.col_ref, bf16[144,1152]{1,0:T(8,128)(2,1)} %select_convert_fusion.3.row_ref), custom_call_target="tpu_custom_call" | custom-call | flops 4246732800 | bytes 9437184 | tf_op jit(solution)/shard_map/synthesis/pallas_call | solution.py:198
  140.1 2.0 fusion.43
  142.0 4.2 %collective-permute-start = (f32[4,144,8]{2,1,0:T(8,128)}, f32[4,144,8]{2,1,0:T(8,128)}, u32[]{:S(2)}, u32[]{:S(2)}) collective-permute-start(f32[4,144,8]{2,1,0:T(8,128)} %get-tuple-element.21), channel_id=1, source_target_pairs={{0,1},{2,3},{4,5},{6,7},{8,9},{10,11},{12,13},{14,15},{16,17},{18,... | collective-permute-start | bytes 55304 | tf_op jit(solution)/shard_map/ppermute | solution.py:265
  147.6 21.2 %all-to-all-done.2 = bf16[32,4,64,128]{3,2,1,0:T(8,128)(2,1)S(1)} async-done(((bf16[32,4,64,128]{3,2,1,0:T(8,128)(2,1)}), bf16[32,4,64,128]{3,2,1,0:T(8,128)(2,1)S(1)}, u32[]{:S(2)}, u32[]{:S(2)}) %all-to-all-start.2) | async-done | bytes 2097184 | tf_op jit(solution)/shard_map/all_to_all | solution.py:348
  170.0 13.8 %backward.1 = bf16[256,2048]{1,0:T(8,128)(2,1)} custom-call(bf16[32,256,128]{2,1,0:T(8,128)(2,1)} %bitcast.145, f32[2048,128]{1,0:T(8,128)} %constant.59.clone.et_ref, f32[2048,128]{1,0:T(8,128)} %constant.72.es_ref, f32[32,32,128]{2,1,0:T(8,128)} %broadcast_in_dim.906.pc_ref, f32[32,32,128]{2,1,0:T(8,128)} %broadcast_in_dim.907.ps_ref), custom_call_target="tpu_custom_call" | custom-call | tf_op jit(solution)/shard_map/backward/pallas_call | solution.py:99
  183.8 2.9 %copy.33 = bf16[4,64,2048]{1,0,2:T(4,128)(2,1)S(1)} copy(bf16[4,64,2048]{2,1,0:T(8,128)(2,1)} %bitcast.150) | data formatting | bytes 2097152 | tf_op jit(solution)/shard_map/reshape | solution.py:354
  186.7 2.4 reshape.214
  189.2 3.6 %all-to-all-start.3 = ((bf16[2,2,131072]{2,1,0:T(2,128)(2,1)}), bf16[2,2,131072]{2,1,0:T(2,128)(2,1)S(1)}, u32[]{:S(2)}, u32[]{:S(2)}) async-start(bf16[2,2,131072]{2,1,0:T(2,128)(2,1)} %reshape.214), calls=%async_computation.3 | async-start | bytes 2097152 | tf_op jit(solution)/shard_map/all_to_all | solution.py:353
  193.0 2.6 fusion
  197.8 1.5 collective-permute-start.3
  211.3 2.3 reshape.215
  213.6 2.9 %copy.34 = bf16[4,64,2048]{2,1,0:T(8,128)(2,1)S(1)} copy(bf16[4,64,2048]{1,0,2:T(4,128)(2,1)} %bitcast.148) | data formatting | bytes 2097152 | tf_op jit(solution)/shard_map/all_to_all | solution.py:353
  216.5 3.1 %reshape.196 = f32[4,64,2,1024]{3,2,1,0:T(2,128)} reshape(bf16[4,64,2048]{2,1,0:T(8,128)(2,1)S(1)} %copy.34) | data formatting | bytes 3145728 | tf_op jit(solution)/shard_map/convert_element_type | solution.py:355
  219.6 2.4 copy.35
  222.4 3.3 %subtract_convert_fusion = (bf16[4,128,1024]{2,1,0:T(8,128)(2,1)S(1)}, f32[4,128,1024]{2,1,0:T(8,128)}) fusion(f32[4,128,1024]{2,1,0:T(8,128)S(1)} %copy-done.3, f32[128]{0:T(128)} %compare_convert_fusion, f32[4,8,1024]{2,1,0:T(8,128)} %collective-permute-done.3, f32[4,8,1024]{2,1,0:T(8,128)S(1)} %collective-permute-done.2, f32[4,144,1024]{2,1,0:T(8,128)S(1)} %fusion, ...), kind=kLoop, calls=%fused_computation.11 | loop fusion | flops 5767168 | bytes 11796992 | tf_op jit(solution)/shard_map/convert_element_type | solution.py:362
  226.0 4.7 %collective-permute-start.4 = (bf16[4,8,1024]{2,1,0:T(8,128)(2,1)S(1)}, bf16[4,8,1024]{2,1,0:T(8,128)(2,1)S(1)}, u32[]{:S(2)}, u32[]{:S(2)}) collective-permute-start(bf16[4,8,1024]{2,1,0:T(8,128)(2,1)S(1)} %get-tuple-element.27), channel_id=1, source_target_pairs={{0,2},{2,4},{4,6},{6,8},{8,10},{10,12},{12,14},{14,16},{16,18},{18... | collective-permute-start | bytes 196616 | tf_op jit(solution)/shard_map/ppermute | solution.py:265
  232.2 3.6 %select_convert_fusion.row_ref = bf16[9,128,144]{2,1,0:T(8,128)(2,1)} fusion(bf16[9]{0:T(256)(128)(2,1)S(1)} %copy-done.99, bf16[9]{0:T(256)(128)(2,1)S(1)} %copy-done.101, bf16[9]{0:T(256)(128)(2,1)S(1)} %copy-done.97, bf16[9]{0:T(256)(128)(2,1)S(1)} %copy-done.95, bf16[9]{0:T(256)(128)(2,1)S(1)} %get-tuple-element.14, ...), kind=kLoop, calls=%fused_computation.13 | loop fusion | flops 2820096 | bytes 645426 | tf_op jit(solution)/shard_map/convert_element_type | solution.py:260
  237.4 4.6 %collective-permute-start.6 = (bf16[4,144,8]{2,1,0:T(8,128)(2,1)S(1)}, bf16[4,144,8]{2,1,0:T(8,128)(2,1)S(1)}, u32[]{:S(2)}, u32[]{:S(2)}) collective-permute-start(bf16[4,144,8]{2,1,0:T(8,128)(2,1)S(1)} %get-tuple-element.26), channel_id=1, source_target_pairs={{0,1},{2,3},{4,5},{6,7},{8,9},{10,11},{12,13},{14,15},{16,17},{18,... | collective-permute-start | bytes 27656 | tf_op jit(solution)/shard_map/ppermute | solution.py:265
  242.2 2.9 %select_convert_fusion.1.col_ref = bf16[9,256,128]{2,1,0:T(8,128)(2,1)} fusion(bf16[9]{0:T(256)(128)(2,1)S(1)} %copy-done.99, bf16[9]{0:T(256)(128)(2,1)S(1)} %copy-done.101, bf16[9]{0:T(256)(128)(2,1)S(1)} %copy-done.97, bf16[9]{0:T(256)(128)(2,1)S(1)} %copy-done.95, bf16[9]{0:T(256)(128)(2,1)S(1)} %get-tuple-element.14, ...), kind=kLoop, calls=%fused_computation.14 | loop fusion | flops 5013504 | bytes 1147186 | tf_op jit(solution)/shard_map/convert_element_type | solution.py:260
  245.1 2.4 concatenate.15.p_ref
  247.5 20.9 %analysis.1 = bf16[4,9,128,1024]{3,2,1,0:T(8,128)(2,1)} custom-call(f32[9]{0:T(128)} %bound_ref.1, bf16[4,144,1152]{2,1,0:T(8,128)(2,1)} %concatenate.15.p_ref, bf16[4,9,128,1024]{3,2,1,0:T(8,128)(2,1)} %d_ref.3, bf16[9,256,128]{2,1,0:T(8,128)(2,1)} %select_convert_fusion.1.col_ref, bf16[9,128,144]{2,1,0:T(8,128)(2,1)} %select_convert_fusion.row_ref), custom_call_target="tpu_custom_call" | custom-call | tf_op jit(solution)/shard_map/analysis/pallas_call | solution.py:237
  (321 shorter events, 32.1 us)
Async XLA Ops:
  0.6 43.1 %copy-start = (bf16[4,2,6,64,64]{4,3,2,1,0:T(8,128)(2,1)S(1)}, bf16[4,2,6,64,64]{4,3,2,1,0:T(8,128)(2,1)}, u32[]{:S(2)}) copy-start(bf16[4,2,6,64,64]{4,3,2,1,0:T(8,128)(2,1)} %param.25) | copy-start | bytes 1179652
  38.6 53.7 %all-to-all-start.1 = ((bf16[32,4,64,128]{3,2,1,0:T(8,128)(2,1)}), bf16[32,4,64,128]{3,2,1,0:T(8,128)(2,1)S(1)}, u32[]{:S(2)}, u32[]{:S(2)}) async-start(bf16[32,4,64,128]{3,2,1,0:T(8,128)(2,1)} %bitcast.146), calls=%async_computation.1 | async-start | bytes 4194304 | tf_op jit(solution)/shard_map/all_to_all | solution.py:305
  116.4 52.3 %all-to-all-start.2 = ((bf16[32,4,64,128]{3,2,1,0:T(8,128)(2,1)}), bf16[32,4,64,128]{3,2,1,0:T(8,128)(2,1)S(1)}, u32[]{:S(2)}, u32[]{:S(2)}) async-start(bf16[32,4,64,128]{3,2,1,0:T(8,128)(2,1)} %gram.1), calls=%async_computation.2 | async-start | bytes 4194304 | tf_op jit(solution)/shard_map/all_to_all | solution.py:348
  142.0 50.9 %collective-permute-start = (f32[4,144,8]{2,1,0:T(8,128)}, f32[4,144,8]{2,1,0:T(8,128)}, u32[]{:S(2)}, u32[]{:S(2)}) collective-permute-start(f32[4,144,8]{2,1,0:T(8,128)} %get-tuple-element.21), channel_id=1, source_target_pairs={{0,1},{2,3},{4,5},{6,7},{8,9},{10,11},{12,13},{14,15},{16,17},{18,... | collective-permute-start | bytes 55304 | tf_op jit(solution)/shard_map/ppermute | solution.py:265
  146.3 46.7 %collective-permute-start.1 = (f32[4,144,8]{2,1,0:T(8,128)}, f32[4,144,8]{2,1,0:T(8,128)}, u32[]{:S(2)}, u32[]{:S(2)}) collective-permute-start(f32[4,144,8]{2,1,0:T(8,128)} %get-tuple-element.22), channel_id=1, source_target_pairs={{1,0},{3,2},{5,4},{7,6},{9,8},{11,10},{13,12},{15,14},{17,16},{19,... | collective-permute-start | bytes 55304 | tf_op jit(solution)/shard_map/ppermute | solution.py:270
  189.2 22.1 %all-to-all-start.3 = ((bf16[2,2,131072]{2,1,0:T(2,128)(2,1)}), bf16[2,2,131072]{2,1,0:T(2,128)(2,1)S(1)}, u32[]{:S(2)}, u32[]{:S(2)}) async-start(bf16[2,2,131072]{2,1,0:T(2,128)(2,1)} %reshape.214), calls=%async_computation.3 | async-start | bytes 2097152 | tf_op jit(solution)/shard_map/all_to_all | solution.py:353
  192.9 16.5 %copy-start.60 = (pred[128,144]{1,0:T(32,128)(4,1)S(1)}, pred[128,144]{1,0:T(32,128)(4,1)}, u32[]{:S(2)}) copy-start(pred[128,144]{1,0:T(32,128)(4,1)} %constant.219) | copy-start | bytes 55300
  192.9 17.1 %copy-start.59 = (pred[128,144]{1,0:T(32,128)(4,1)S(1)}, pred[128,144]{1,0:T(32,128)(4,1)}, u32[]{:S(2)}) copy-start(pred[128,144]{1,0:T(32,128)(4,1)} %constant.220) | copy-start | bytes 55300
  196.3 25.8 %collective-permute-start.2 = (f32[4,8,1024]{2,1,0:T(8,128)}, f32[4,8,1024]{2,1,0:T(8,128)S(1)}, u32[]{:S(2)}, u32[]{:S(2)}) collective-permute-start(f32[4,8,1024]{2,1,0:T(8,128)} %get-tuple-element.23), channel_id=1, source_target_pairs={{0,2},{2,4},{4,6},{6,8},{8,10},{10,12},{12,14},{14,16},{16,18},{18... | collective-permute-start | bytes 393224 | tf_op jit(solution)/shard_map/ppermute | solution.py:265
  197.8 24.4 %collective-permute-start.3 = (f32[4,8,1024]{2,1,0:T(8,128)}, f32[4,8,1024]{2,1,0:T(8,128)}, u32[]{:S(2)}, u32[]{:S(2)}) collective-permute-start(f32[4,8,1024]{2,1,0:T(8,128)} %get-tuple-element.24), channel_id=1, source_target_pairs={{2,0},{4,2},{6,4},{8,6},{10,8},{12,10},{14,12},{16,14},{18,16},{20... | collective-permute-start | bytes 393224 | tf_op jit(solution)/shard_map/ppermute | solution.py:270
  225.8 16.2 %copy-start.25 = (pred[256,128]{1,0:T(32,128)(4,1)S(1)}, pred[256,128]{1,0:T(32,128)(4,1)}, u32[]{:S(2)}) copy-start(pred[256,128]{1,0:T(32,128)(4,1)} %constant.203) | copy-start | bytes 98308
  225.8 16.2 %copy-start.26 = (pred[256,128]{1,0:T(32,128)(4,1)S(1)}, pred[256,128]{1,0:T(32,128)(4,1)}, u32[]{:S(2)}) copy-start(pred[256,128]{1,0:T(32,128)(4,1)} %constant.202) | copy-start | bytes 98308
  225.8 16.2 %copy-start.27 = (pred[256,128]{1,0:T(32,128)(4,1)S(1)}, pred[256,128]{1,0:T(32,128)(4,1)}, u32[]{:S(2)}) copy-start(pred[256,128]{1,0:T(32,128)(4,1)} %constant.201) | copy-start | bytes 98308
  225.8 16.2 %copy-start.28 = (pred[256,128]{1,0:T(32,128)(4,1)S(1)}, pred[256,128]{1,0:T(32,128)(4,1)}, u32[]{:S(2)}) copy-start(pred[256,128]{1,0:T(32,128)(4,1)} %constant.200) | copy-start | bytes 98308
  225.8 16.2 %copy-start.29 = (pred[256,128]{1,0:T(32,128)(4,1)S(1)}, pred[256,128]{1,0:T(32,128)(4,1)}, u32[]{:S(2)}) copy-start(pred[256,128]{1,0:T(32,128)(4,1)} %constant.199) | copy-start | bytes 98308
  225.8 16.2 %copy-start.30 = (pred[256,128]{1,0:T(32,128)(4,1)S(1)}, pred[256,128]{1,0:T(32,128)(4,1)}, u32[]{:S(2)}) copy-start(pred[256,128]{1,0:T(32,128)(4,1)} %constant.198) | copy-start | bytes 98308
  225.8 16.2 %copy-start.31 = (pred[256,128]{1,0:T(32,128)(4,1)S(1)}, pred[256,128]{1,0:T(32,128)(4,1)}, u32[]{:S(2)}) copy-start(pred[256,128]{1,0:T(32,128)(4,1)} %constant.197) | copy-start | bytes 98308
  225.8 16.2 %copy-start.32 = (pred[256,128]{1,0:T(32,128)(4,1)S(1)}, pred[256,128]{1,0:T(32,128)(4,1)}, u32[]{:S(2)}) copy-start(pred[256,128]{1,0:T(32,128)(4,1)} %constant.196) | copy-start | bytes 98308
  225.9 16.1 %copy-start.33 = (pred[256,128]{1,0:T(32,128)(4,1)S(1)}, pred[256,128]{1,0:T(32,128)(4,1)}, u32[]{:S(2)}) copy-start(pred[256,128]{1,0:T(32,128)(4,1)} %constant.195) | copy-start | bytes 98308
  225.9 16.1 %copy-start.34 = (pred[256,128]{1,0:T(32,128)(4,1)S(1)}, pred[256,128]{1,0:T(32,128)(4,1)}, u32[]{:S(2)}) copy-start(pred[256,128]{1,0:T(32,128)(4,1)} %constant.194) | copy-start | bytes 98308
  225.9 16.1 %copy-start.35 = (pred[256,128]{1,0:T(32,128)(4,1)S(1)}, pred[256,128]{1,0:T(32,128)(4,1)}, u32[]{:S(2)}) copy-start(pred[256,128]{1,0:T(32,128)(4,1)} %constant.193) | copy-start | bytes 98308
  225.9 16.1 %copy-start.36 = (pred[256,128]{1,0:T(32,128)(4,1)S(1)}, pred[256,128]{1,0:T(32,128)(4,1)}, u32[]{:S(2)}) copy-start(pred[256,128]{1,0:T(32,128)(4,1)} %constant.192) | copy-start | bytes 98308
  225.9 16.1 %copy-start.37 = (pred[256,128]{1,0:T(32,128)(4,1)S(1)}, pred[256,128]{1,0:T(32,128)(4,1)}, u32[]{:S(2)}) copy-start(pred[256,128]{1,0:T(32,128)(4,1)} %constant.191) | copy-start | bytes 98308
  225.9 16.1 %copy-start.38 = (pred[256,128]{1,0:T(32,128)(4,1)S(1)}, pred[256,128]{1,0:T(32,128)(4,1)}, u32[]{:S(2)}) copy-start(pred[256,128]{1,0:T(32,128)(4,1)} %constant.190) | copy-start | bytes 98308
  225.9 16.1 %copy-start.39 = (pred[256,128]{1,0:T(32,128)(4,1)S(1)}, pred[256,128]{1,0:T(32,128)(4,1)}, u32[]{:S(2)}) copy-start(pred[256,128]{1,0:T(32,128)(4,1)} %constant.189) | copy-start | bytes 98308
  225.9 16.1 %copy-start.40 = (pred[256,128]{1,0:T(32,128)(4,1)S(1)}, pred[256,128]{1,0:T(32,128)(4,1)}, u32[]{:S(2)}) copy-start(pred[256,128]{1,0:T(32,128)(4,1)} %constant.188) | copy-start | bytes 98308
  226.0 16.1 %copy-start.41 = (pred[256,128]{1,0:T(32,128)(4,1)S(1)}, pred[256,128]{1,0:T(32,128)(4,1)}, u32[]{:S(2)}) copy-start(pred[256,128]{1,0:T(32,128)(4,1)} %constant.187) | copy-start | bytes 98308
  226.0 9.8 %collective-permute-start.4 = (bf16[4,8,1024]{2,1,0:T(8,128)(2,1)S(1)}, bf16[4,8,1024]{2,1,0:T(8,128)(2,1)S(1)}, u32[]{:S(2)}, u32[]{:S(2)}) collective-permute-start(bf16[4,8,1024]{2,1,0:T(8,128)(2,1)S(1)} %get-tuple-element.27), channel_id=1, source_target_pairs={{0,2},{2,4},{4,6},{6,8},{8,10},{10,12},{12,14},{14,16},{16,18},{18... | collective-permute-start | bytes 196616 | tf_op jit(solution)/shard_map/ppermute | solution.py:265
  230.7 5.1 %collective-permute-start.5 = (bf16[4,8,1024]{2,1,0:T(8,128)(2,1)S(1)}, bf16[4,8,1024]{2,1,0:T(8,128)(2,1)S(1)}, u32[]{:S(2)}, u32[]{:S(2)}) collective-permute-start(bf16[4,8,1024]{2,1,0:T(8,128)(2,1)S(1)} %get-tuple-element.28), channel_id=1, source_target_pairs={{2,0},{4,2},{6,4},{8,6},{10,8},{12,10},{14,12},{16,14},{18,16},{20... | collective-permute-start | bytes 196616 | tf_op jit(solution)/shard_map/ppermute | solution.py:270
  236.1 9.0 %collective-permute-start.7 = (bf16[4,144,8]{2,1,0:T(8,128)(2,1)S(1)}, bf16[4,144,8]{2,1,0:T(8,128)(2,1)S(1)}, u32[]{:S(2)}, u32[]{:S(2)}) collective-permute-start(bf16[4,144,8]{2,1,0:T(8,128)(2,1)S(1)} %get-tuple-element.25), channel_id=1, source_target_pairs={{1,0},{3,2},{5,4},{7,6},{9,8},{11,10},{13,12},{15,14},{17,16},{19,... | collective-permute-start | bytes 27656 | tf_op jit(solution)/shard_map/ppermute | solution.py:270
  237.4 7.7 %collective-permute-start.6 = (bf16[4,144,8]{2,1,0:T(8,128)(2,1)S(1)}, bf16[4,144,8]{2,1,0:T(8,128)(2,1)S(1)}, u32[]{:S(2)}, u32[]{:S(2)}) collective-permute-start(bf16[4,144,8]{2,1,0:T(8,128)(2,1)S(1)} %get-tuple-element.26), channel_id=1, source_target_pairs={{0,1},{2,3},{4,5},{6,7},{8,9},{10,11},{12,13},{14,15},{16,17},{18,... | collective-permute-start | bytes 27656 | tf_op jit(solution)/shard_map/ppermute | solution.py:265
  247.5 21.0 %copy-start.1 = (bf16[4,2,6,64,64]{4,3,2,1,0:T(8,128)(2,1)S(1)}, bf16[4,2,6,64,64]{4,3,2,1,0:T(8,128)(2,1)}, u32[]{:S(2)}) copy-start(bf16[4,2,6,64,64]{4,3,2,1,0:T(8,128)(2,1)} %param.25) | copy-start | bytes 1179652
  (101 other events, 728.4 us)
where the time goes:
time: 272 us; the launch traced here: 268 us
  Pallas kernels  81.2 us (30%)
  waiting for transfers between devices  60.9 us (22%)
  local copies, waits for them, and re-layouts  52.7 us (19%)
  starting transfers between devices  32.8 us (12%)
  other arithmetic  20 us (7%)
  blocking collectives  17.7 us (7%)
  between operations  3.28 us (1%)
    all_to_all x1, waiting for transfers between devices, body(): lax.all_to_all(spread, axes, split_axis=0, concat_axis=0, tiled=True)  39.7 us
    unnamed x266, local copies, waits for them, and re-layouts  23.5 us
    pallas_call x1, Pallas kernels, gram(): pl.pallas_call(gram_kernel, grid_spec=pltpu.PrefetchScalarGridSpec(num_sc...  22.5 us
    all_to_all x1, waiting for transfers between devices, body(): back = lax.all_to_all(y, axes, split_axis=0, concat_axis=0, tiled=True)  21.2 us
    pallas_call x1, Pallas kernels, analyse(): pl.pallas_call(analysis_kernel, grid=(frames,), in_specs=[pl.BlockSpec(me...  20.9 us
    all_to_all x1, blocking collectives, body(): lax.all_to_all(sky.astype(BF16), 'fou', split_axis=1, concat_axis=2, tile...  17.7 us
    ppermute x4, starting transfers between devices, shift_up(): return lax.ppermute(x, axis, [(i, i + 1) for i in range(count - 1)])  14.9 us
    pallas_call x1, Pallas kernels, backward(): pl.pallas_call(functools.partial(backward_kernel, scale), grid=(line // p...  13.8 us
  transfers between devices with their start and end apart: 11, of which 2 were waited for; matrix products, arithmetic and copies ran while one was open for 21% of the time, Pallas kernels for 9%

commit v1 on v0

--- a/solution.py
+++ b/solution.py
@@ -270,6 +270,618 @@
     return lax.ppermute(x, axis, [(i + 1, i) for i in range(count - 1)])
 
 
+MESH = pl.DeviceIdType.MESH
+HIGH = lax.Precision.HIGHEST
+NT = ((1,), (1,))
+TN = ((0,), (0,))
+
+
+def lane_ids(rows, lanes):
+    return lax.broadcasted_iota(jnp.int32, (rows, lanes), 1)
+
+
+def swap(x):
+    return pltpu.roll(x, x.shape[1] // 2, 1)
+
+
+def split(x):
+    high = x.astype(BF16).astype(F32)
+    return high, x - high
+
+
+def fft(xs, sign, side):
+    n = len(xs)
+    if n == 1:
+        return xs
+    even, odd = fft(xs[::2], sign, side), fft(xs[1::2], sign, side)
+    low, high = [], []
+    for k in range(n // 2):
+        angle = sign * 2.0 * math.pi * k / n
+        c, s = math.cos(angle), math.sin(angle)
+        t = odd[k]
+        if 4 * k == n:
+            t = swap(t) * (side * s)
+        elif k:
+            t = t * c + swap(t) * (side * s)
+        low.append(even[k] + t)
+        high.append(even[k] - t)
+    return low + high
+
+
+def core_tables(line, n, block, slots):
+    rows = line // n
+    lanes = 2 * block
+    tiles = line // block
+    taps = block // n
+
+    def trig(product, period):
+        angle = (product % period) * (2.0 * math.pi / period)
+        return np.cos(angle), np.sin(angle)
+
+    s = np.arange(line)
+    c, sn = trig(s[:, None] * np.arange(block)[None, :], line)
+    base = np.concatenate([c, -sn], axis=1)
+    c, sn = trig(np.arange(n)[:, None] * np.arange(n)[None, :], n)
+    turn_c = np.broadcast_to(c[:, :, None], (n, n, lanes))
+    turn_s = np.broadcast_to(sn[:, :, None], (n, n, lanes))
+    small_c = np.zeros((n, lanes))
+    small_s = np.zeros((n, lanes))
+    small_c[:, :n], small_s[:, :n] = c, sn
+    pair_c, pair_s = small_c.copy(), small_s.copy()
+    pair_c[:, n : 2 * n], pair_s[:, n : 2 * n] = c, sn
+    c, sn = trig((np.arange(n) * 2 + 1)[:, None] * block * s[None, :], line)
+    edge = np.concatenate([c, -sn], axis=0)
+    r = np.arange(rows)
+    u = np.arange(n)[:, None] + n * np.arange(taps)[None, :]
+    c, sn = trig(u[:, :, None] * r[None, None, :], line)
+    real = np.concatenate([c, sn], axis=2)
+    imag = np.concatenate([-sn, c], axis=2)
+    phase = np.concatenate([real, imag], axis=1)
+    phase2 = np.concatenate([imag, -real], axis=1)
+    c, sn = trig(np.arange(tiles)[:, None] * block * r[None, :], line)
+    tile_c = np.zeros((lanes, 2 * rows))
+    tile_s = np.zeros((lanes, 2 * rows))
+    tile_c[:tiles] = np.concatenate([c, c], axis=1)
+    tile_s[:tiles] = np.concatenate([sn, sn], axis=1)
+    where_row = np.arange(2 * block)
+    b = where_row // (2 * taps) + n * (where_row % taps)
+    pick = (b[:, None] == np.arange(block)[None, :]).astype(np.float64)
+    part = where_row // taps % 2
+    same = (part[:, None] == part[None, :]).astype(np.float64)
+    f32 = [base, turn_c, turn_s, small_c, small_s, pair_c, pair_s, phase, phase2, tile_c, tile_s, same]
+    bf16 = [edge, pick, pick.T]
+    return [np.ascontiguousarray(a, dtype=np.float32) for a in f32] + [
+        np.ascontiguousarray(a, dtype=np.float32).astype(BF16) for a in bf16
+    ]
+
+
+def core_kernel(scale, sky, gram, slot, base, turn_c, turn_s, small_c, small_s, pair_c, pair_s,
+                phase, phase2, tile_c, tile_s, same, edge, pick, pick_t, out,
+                table, held, lines, sent, got, sent_e, got_e, gram_far, slot_far, left, right, tail,
+                grow_c, grow_s, mid, wide, tail_sum, back, back_e, home, home_e, half, half_got,
+                near_s, near_r, far_s, far_r, fwd_s, fwd_r, edge_s, edge_r, bwd_s, bwd_r,
+                bedge_s, bedge_r, last_s, last_r):
+    n, fou = lax.axis_size("img"), lax.axis_size("fou")
+    devices = n * fou
+    i, f = lax.axis_index("img"), lax.axis_index("fou")
+    me = i * fou + f
+    other = 1 - f
+    partner = n - 1 - i
+    chunks = lines.shape[0]
+    rows, cols = sky.shape[1], sky.shape[2]
+    slab = rows // fou
+    lanes = base.shape[1]
+    block = lanes // 2
+    taps = block // n
+    slots = gram.shape[2]
+    line = cols * fou
+    low = lane_ids(1, lanes) < block
+    side = jnp.where(low, -1.0, 1.0).astype(F32)
+    edge_lane = lane_ids(1, lanes) % block == 0
+    all_lane = lane_ids(1, lanes)
+
+    barrier = pltpu.get_barrier_semaphore()
+
+    def greet(k, _):
+        peer = (me + k) % devices
+        pl.semaphore_signal(barrier, inc=1, device_id=(peer // fou, peer % fou), device_id_type=MESH)
+        return 0
+
+    lax.fori_loop(1, devices, greet, 0)
+
+    def stage(p, _):
+        mine = pl.ds(pl.multiple_of(f * slab, slab), slab)
+        theirs = pl.ds(pl.multiple_of(other * slab, slab), slab)
+        here = pl.ds(pl.multiple_of(f * cols, cols), cols)
+        for q in range(fou):
+            held[p, q * slab : (q + 1) * slab, :] = sky[p * fou + q, theirs, :].astype(BF16)
+            lines[p, q * slab : (q + 1) * slab, here] = sky[p * fou + q, mine, :].astype(BF16)
+        return 0
+
+    lax.fori_loop(0, chunks, stage, 0)
+    pl.semaphore_wait(barrier, devices - 1)
+
+    def near_copy(p):
+        here = pl.ds(pl.multiple_of(f * cols, cols), cols)
+        return pltpu.make_async_remote_copy(
+            src_ref=held.at[p], dst_ref=lines.at[p, :, here], send_sem=near_s.at[p],
+            recv_sem=near_r.at[p], device_id=(i, other), device_id_type=MESH)
+
+    def far_copies(p):
+        return [
+            pltpu.make_async_remote_copy(
+                src_ref=gram.at[p * fou + f, 1], dst_ref=gram_far.at[p], send_sem=far_s.at[p, 0],
+                recv_sem=far_r.at[p, 0], device_id=(partner, f), device_id_type=MESH),
+            pltpu.make_async_remote_copy(
+                src_ref=slot.at[p * fou + f, 1], dst_ref=slot_far.at[p], send_sem=far_s.at[p, 1],
+                recv_sem=far_r.at[p, 1], device_id=(partner, f), device_id_type=MESH),
+        ]
+
+    def open_sends(p, _):
+        near_copy(p).start()
+        return 0
+
+    def open_far(p, _):
+        for copy in far_copies(p):
+            copy.start()
+        return 0
+
+    lax.fori_loop(0, chunks, open_sends, 0)
+    lax.fori_loop(0, chunks, open_far, 0)
+
+    period = turn_c.shape[1]
+    shape = (rows // period, period, lanes)
+
+    def other_base(a, _):
+        at = pl.ds(pl.multiple_of(a * rows, rows), rows)
+        wide[a] = swap(base[at, :]) * -side
+        return 0
+
+    lax.fori_loop(0, n, other_base, 0)
+
+    def fill(t, _):
+        to = pl.ds(pl.multiple_of(t * lanes, lanes), lanes)
+        c, s = turn_c[t][None], turn_s[t][None]
+
+        def piece(a, _):
+            at = pl.ds(pl.multiple_of(a * rows, rows), rows)
+            value = base[at, :].reshape(shape) * c + wide[a].reshape(shape) * s
+            table[at, to] = value.reshape(rows, lanes).astype(BF16)
+            return 0
+
+        lax.fori_loop(0, n, piece, 0)
+        return 0
+
+    lax.fori_loop(0, n, fill, 0)
+
+    def fwd_copy(p, t, q):
+        return pltpu.make_async_remote_copy(
+            src_ref=sent.at[p, pl.ds(pl.multiple_of(q * slab, slab), slab), pl.ds(pl.multiple_of(t * lanes, lanes), lanes)],
+            dst_ref=got.at[p, i, pl.ds(pl.multiple_of(f * slab, slab), slab), :],
+            send_sem=fwd_s.at[p, t * fou + q], recv_sem=fwd_r.at[p, me],
+            device_id=(t, q), device_id_type=MESH)
+
+    def edge_copy(p, t, q):
+        return pltpu.make_async_remote_copy(
+            src_ref=sent_e.at[p, q, t], dst_ref=got_e.at[p, f, i],
+            send_sem=edge_s.at[p, t * fou + q], recv_sem=edge_r.at[p, me],
+            device_id=(t, q), device_id_type=MESH)
+
+    def bwd_copy(p, t, q):
+        return pltpu.make_async_remote_copy(
+            src_ref=back.at[p, t, pl.ds(pl.multiple_of(q * slab, slab), slab), :],
+            dst_ref=home.at[p, pl.ds(pl.multiple_of(f * slab, slab), slab),
+                            pl.ds(pl.multiple_of(i * lanes, lanes), lanes)],
+            send_sem=bwd_s.at[p, t * fou + q], recv_sem=bwd_r.at[p, me],
+            device_id=(t, q), device_id_type=MESH)
+
+    def bedge_copy(p, t, q):
+        return pltpu.make_async_remote_copy(
+            src_ref=back_e.at[p, q, t], dst_ref=home_e.at[p, f, i],
+            send_sem=bedge_s.at[p, t * fou + q], recv_sem=bedge_r.at[p, me],
+            device_id=(t, q), device_id_type=MESH)
+
+    pairs = n // 2
+
+    def forward_chunk(p, _):
+        near_copy(p).wait_recv()
+        x = lines[p]
+
+        def tile(m, _):
+            g = (i // 2 + pairs // 2 + m) % pairs
+            at = pl.ds(pl.multiple_of(g * 2 * lanes, 2 * lanes), 2 * lanes)
+            sent[p, :, at] = dot(lines[p], table[:, at]).astype(BF16)
+            for a in range(2):
+                for q in range(fou):
+                    t = g * 2 + a
+                    itself = (t == i) & (q == f)
+
+                    @pl.when(jnp.logical_not(itself))
+                    def _():
+                        fwd_copy(p, t, q).start()
+
+                    @pl.when(itself)
+                    def _():
+                        got[p, i, pl.ds(pl.multiple_of(f * slab, slab), slab), :] = sent[
+                            p, q * slab : (q + 1) * slab, pl.ds(pl.multiple_of(t * lanes, lanes), lanes)]
+            return 0
+
+        lax.fori_loop(0, pairs, tile, 0)
+        e = dot(edge[...], x, NT)
+        er, ei = e[:n], e[n:]
+        for q in range(fou):
+            both = jnp.where(low, er, swap(ei)) if q == 0 else jnp.where(low, swap(er), ei)
+            for t in range(n):
+                sent_e[p, q, t] = both[t : t + 1]
+
+        def send_edges(k, _):
+            peer = (me + k) % devices
+            edge_copy(p, peer // fou, peer % fou).start()
+            return 0
+
+        lax.fori_loop(1, devices, send_edges, 0)
+        got_e[p, f, i] = sent_e[p, f, i]
+        return 0
+
+    lax.fori_loop(0, chunks, forward_chunk, 0)
+
+    step = 16
+
+    def gram_chunk(p, _):
+        def arrive(k, _):
+            peer = (me + k) % devices
+            pltpu.make_async_remote_copy(
+                src_ref=sent.at[p, 0:slab, 0:lanes],
+                dst_ref=got.at[p, peer // fou, pl.ds(pl.multiple_of(peer % fou * slab, slab), slab), :],
+                send_sem=fwd_s.at[p, peer], recv_sem=fwd_r.at[p, peer],
+                device_id=(peer // fou, peer % fou), device_id_type=MESH).wait_recv()
+            pltpu.make_async_remote_copy(
+                src_ref=sent_e.at[p, 0, 0], dst_ref=got_e.at[p, peer % fou, peer // fou],
+                send_sem=edge_s.at[p, peer], recv_sem=edge_r.at[p, peer],
+                device_id=(peer // fou, peer % fou), device_id_type=MESH).wait_recv()
+            return 0
+
+        lax.fori_loop(1, devices, arrive, 0)
+
+        def column(m, _):
+            at = pl.ds(pl.multiple_of(m * step, step), step)
+            below = pl.ds(pl.multiple_of(rows + m * step, step), step)
+            xs = [got[p, t, at, :].astype(F32) for t in range(n)]
+            for t, a in enumerate(fft(xs, -1.0, side)):
+                high, rest = split(a)
+                right[t, at, :] = jnp.where(low, high, swap(rest)).astype(BF16)
+                right[t, below, :] = jnp.where(low, swap(high), rest).astype(BF16)
+            return 0
+
+        lax.fori_loop(0, rows // step, column, 0)
+        e0 = jnp.concatenate([got_e[p, 0, t] for t in range(n)], axis=0)
+        e1 = jnp.concatenate([got_e[p, 1, t] for t in range(n)], axis=0)
+        zr = jnp.where(low, e0, swap(e1))
+        zi = jnp.where(low, swap(e0), e1)
+        for part in range(2):
+            if part == 0:
+                a = dot(zr, pair_c[...], TN, precision=HIGH) + dot(zi, pair_s[...], TN, precision=HIGH)
+            else:
+                a = dot(zi, pair_c[...], TN, precision=HIGH) - dot(zr, pair_s[...], TN, precision=HIGH)
+            high, rest = split(a)
+            tail[part * rows : (part + 1) * rows] = jnp.where(all_lane < n, high, rest).astype(BF16)
+
+        for copy in far_copies(p):
+            copy.wait_recv()
+        for far in range(2):
+            t = slot_far[p] if far else slot[p * fou + f, 0]
+            hot = jnp.where(t == lane_ids(*t.shape).astype(F32), 1.0, 0.0)
+            gc = dot(hot, tile_c[...], precision=HIGH)
+            gs = dot(hot, tile_s[...], precision=HIGH)
+            for k in range(slots):
+                grow_c[far, k] = jnp.broadcast_to(gc[k : k + 1], (2 * taps, 2 * rows))
+                grow_s[far, k] = jnp.broadcast_to(gs[k : k + 1], (2 * taps, 2 * rows))
+
+        mirror = jnp.where(lane_ids(1, 2 * rows) < rows, 1.0, -1.0).astype(F32)
+        deep = slots * 2 * taps
+
+        def project(b, _):
+            nb = (n - b) % n
+            near = phase[b][None] * grow_c[0] + phase2[b][None] * grow_s[0]
+            far = ((phase[nb] * mirror)[None] * grow_c[1] + (phase2[nb] * mirror)[None] * grow_s[1])
+            left[b, :deep] = near.reshape(deep, 2 * rows).astype(BF16)
+            left[b, deep:] = far.reshape(deep, 2 * rows).astype(BF16)
+            both = dot(left[b], jnp.concatenate([right[b], tail[...]], axis=1))
+            main = both[:, :lanes]
+            main = main + swap(main)
+            hit = (all_lane == b) | (all_lane == n + b)
+            column = jnp.sum(jnp.where(hit, both[deep:, lanes:], 0.0), axis=1, keepdims=True)
+            mirrored = jnp.where(edge_lane, column, main[deep:])
+            width = 2 * taps
+            mid[:slots, pl.ds(pl.multiple_of(b * width, width), width), :] = main[:deep].reshape(slots, width, lanes)
+            mid[slots:, pl.ds(pl.multiple_of(nb * width, width), width), :] = mirrored.reshape(slots, width, lanes)
+            return 0
+
+        lax.fori_loop(0, n, project, 0)
+
+        def weigh(k, far):
+            g = gram_far[p, k] if far else gram[p * fou + f, 0, k]
+            g = dot(pick[...], g, NT).astype(BF16)
+            g = (dot(g, pick_t[...]) * same[...]).astype(BF16)
+            at = slots + k if far else k
+            high, rest = split(mid[at])
+            w = dot(g, jnp.where(low, high, rest).astype(BF16))
+            mid[at] = w + swap(w)
+
+        for far in range(2):
+            lax.fori_loop(0, slots, lambda k, _, far=far: (weigh(k, far), 0)[1], 0)
+
+        tail_sum[...] = jnp.zeros_like(tail_sum)
+
+        def spread(b, _):
+            nb = (n - b) % n
+            width = 2 * taps
+            near = mid[:slots, pl.ds(pl.multiple_of(b * width, width), width), :].reshape(deep, lanes)
+            far = mid[slots:, pl.ds(pl.multiple_of(nb * width, width), width), :].reshape(deep, lanes)
+            column = far[:, 0:1]
+            ch, cr = split(column)
+            extra = jnp.where(all_lane == b, ch, jnp.where(all_lane == n + b, cr, 0.0))
+            both = jnp.concatenate([near, jnp.where(edge_lane, 0.0, far)], axis=0)
+            high, rest = split(both)
+            extra = jnp.concatenate([jnp.zeros((deep, lanes), F32), extra], axis=0)
+            rhs = jnp.concatenate([jnp.where(low, high, rest), extra], axis=1).astype(BF16)
+            y = dot(left[b], rhs, TN)
+            main = y[:, :lanes]
+            main = main + swap(main)
+            wide[b] = jnp.where(low, main[:rows], main[rows:])
+            tail_sum[...] += y[:, lanes:]
+            return 0
+
+        lax.fori_loop(0, n, spread, 0)
+
+        def uncolumn(m, _):
+            at = pl.ds(pl.multiple_of(m * step, step), step)
+            for t, a in enumerate(fft([wide[b, at, :] for b in range(n)], 1.0, side)):
+                back[p, t, at, :] = a.astype(BF16)
+            return 0
+
+        lax.fori_loop(0, rows // step, uncolumn, 0)
+        total = tail_sum[...]
+        total = total + pltpu.roll(total, lanes - n, 1)
+        br, bi = total[:rows], total[rows:]
+        yr = dot(small_c[...], br, NT, precision=HIGH) - dot(small_s[...], bi, NT, precision=HIGH)
+        yi = dot(small_s[...], br, NT, precision=HIGH) + dot(small_c[...], bi, NT, precision=HIGH)
+        for q in range(fou):
+            both = jnp.where(low, yr, swap(yi)) if q == 0 else jnp.where(low, swap(yr), yi)
+            for t in range(n):
+                back_e[p, q, t] = both[t : t + 1]
+
+        def send_back(k, _):
+            peer = (me + devices // 2 + k) % devices
+            t, q = peer // fou, peer % fou
+
+            @pl.when(peer != me)
+            def _():
+                bwd_copy(p, t, q).start()
+                bedge_copy(p, t, q).start()
+
+            return 0
+
+        lax.fori_loop(0, devices, send_back, 0)
+        home[p, pl.ds(pl.multiple_of(f * slab, slab), slab), pl.ds(pl.multiple_of(i * lanes, lanes), lanes)] = back[
+            p, i, pl.ds(pl.multiple_of(f * slab, slab), slab), :]
+        home_e[p, f, i] = back_e[p, f, i]
+        return 0
+
+    lax.fori_loop(0, chunks, gram_chunk, 0)
+
+    def half_copy(p):
+        return pltpu.make_async_remote_copy(
+            src_ref=half.at[p], dst_ref=half_got.at[p], send_sem=last_s.at[p],
+            recv_sem=last_r.at[p], device_id=(i, other), device_id_type=MESH)
+
+    def backward_chunk(p, _):
+        def arrive(k, _):
+            peer = (me + k) % devices
+            pltpu.make_async_remote_copy(
+                src_ref=back.at[p, 0, 0:slab, :],
+                dst_ref=home.at[p, pl.ds(pl.multiple_of(peer % fou * slab, slab), slab),
+                                pl.ds(pl.multiple_of(peer // fou * lanes, lanes), lanes)],
+                send_sem=bwd_s.at[p, peer], recv_sem=bwd_r.at[p, peer],
+                device_id=(peer // fou, peer % fou), device_id_type=MESH).wait_recv()
+            pltpu.make_async_remote_copy(
+                src_ref=back_e.at[p, 0, 0], dst_ref=home_e.at[p, peer % fou, peer // fou],
+                send_sem=bedge_s.at[p, peer], recv_sem=bedge_r.at[p, peer],
+                device_id=(peer // fou, peer % fou), device_id_type=MESH).wait_recv()
+            return 0
+
+        lax.fori_loop(1, devices, arrive, 0)
+        e0 = jnp.concatenate([home_e[p, 0, t] for t in range(n)], axis=0)
+        e1 = jnp.concatenate([home_e[p, 1, t] for t in range(n)], axis=0)
+        ext = jnp.concatenate(
+            [jnp.where(low, e0, swap(e1)), jnp.where(low, swap(e0), e1)], axis=0).astype(BF16)
+        part = 256
+
+        def image(start):
+            at = pl.ds(pl.multiple_of(start, part), part)
+            y = dot(home[p], table[at, :], NT) + dot(ext, edge[:, at], TN)
+            return y * scale
+
+        def send_half(m, _):
+            to = pl.ds(pl.multiple_of(m * part, part), part)
+            half[p, :, to] = image(other * cols + m * part).astype(BF16)
+            return 0
+
+        lax.fori_loop(0, cols // part, send_half, 0)
+        half_copy(p).start()
+
+        def keep_half(m, _):
+            to = pl.ds(pl.multiple_of(m * part, part), part)
+            y = image(f * cols + m * part)
+            for q in range(fou):
+                out[p * fou + q, pl.ds(pl.multiple_of(f * slab, slab), slab), to] = y[q * slab : (q + 1) * slab]
+            return 0
+
+        lax.fori_loop(0, cols // part, keep_half, 0)
+        return 0
+
+    lax.fori_loop(0, chunks, backward_chunk, 0)
+
+    def close(p, _):
+        half_copy(p).wait_recv()
+        for q in range(fou):
+            out[p * fou + q, pl.ds(pl.multiple_of(other * slab, slab), slab), :] = half_got[
+                p, q * slab : (q + 1) * slab, :].astype(F32)
+        half_copy(p).wait_send()
+        near_copy(p).wait_send()
+        for copy in far_copies(p):
+            copy.wait_send()
+
+        def sent_all(k, _):
+            peer = (me + k) % devices
+            pltpu.make_async_remote_copy(
+                src_ref=sent.at[p, 0:slab, 0:lanes], dst_ref=got.at[p, 0, 0:slab, :],
+                send_sem=fwd_s.at[p, peer], recv_sem=fwd_r.at[p, peer],
+                device_id=(peer // fou, peer % fou), device_id_type=MESH).wait_send()
+            pltpu.make_async_remote_copy(
+                src_ref=sent_e.at[p, 0, 0], dst_ref=got_e.at[p, 0, 0],
+                send_sem=edge_s.at[p, peer], recv_sem=edge_r.at[p, peer],
+                device_id=(peer // fou, peer % fou), device_id_type=MESH).wait_send()
+            pltpu.make_async_remote_copy(
+                src_ref=back.at[p, 0, 0:slab, :], dst_ref=home.at[p, 0:slab, 0:lanes],
+                send_sem=bwd_s.at[p, peer], recv_sem=bwd_r.at[p, peer],
+                device_id=(peer // fou, peer % fou), device_id_type=MESH).wait_send()
+            pltpu.make_async_remote_copy(
+                src_ref=back_e.at[p, 0, 0], dst_ref=home_e.at[p, 0, 0],
+                send_sem=bedge_s.at[p, peer], recv_sem=bedge_r.at[p, peer],
+                device_id=(peer // fou, peer % fou), device_id_type=MESH).wait_send()
+            return 0
+
+        lax.fori_loop(1, devices, sent_all, 0)
+        return 0
+
+    lax.fori_loop(0, chunks, close, 0)
+
+
+def core(sky, gram, slot, line, n, fou, block):
+    channels, rows, cols = sky.shape
+    chunks = channels // fou
+    slab = rows // fou
+    lanes = 2 * block
+    devices = n * fou
+    slots = gram.shape[2]
+    taps = block // n
+    consts = core_tables(line, n, block, slots)
+    vm = pl.BlockSpec(memory_space=pltpu.VMEM)
+    dma = pltpu.SemaphoreType.DMA
+    return pl.pallas_call(
+        functools.partial(core_kernel, 1.0 / float(line * line)),
+        in_specs=[vm] * (3 + len(consts)),
+        out_specs=vm,
+        out_shape=jax.ShapeDtypeStruct(sky.shape, F32),
+        scratch_shapes=[
+            pltpu.VMEM((line, line), BF16),
+            pltpu.VMEM((chunks, fou * slab, cols), BF16),
+            pltpu.VMEM((chunks, fou * slab, line), BF16),
+            pltpu.VMEM((chunks, fou * slab, line), BF16),
+            pltpu.VMEM((chunks, n, rows, lanes), BF16),
+            pltpu.VMEM((chunks, fou, n, 1, lanes), F32),
+            pltpu.VMEM((chunks, fou, n, 1, lanes), F32),
+            pltpu.VMEM((chunks,) + gram.shape[2:], BF16),
+            pltpu.VMEM((chunks,) + slot.shape[2:], F32),
+            pltpu.VMEM((n, slots * 4 * taps, 2 * rows), BF16),
+            pltpu.VMEM((n, 2 * rows, lanes), BF16),
+            pltpu.VMEM((2 * rows, lanes), BF16),
+            pltpu.VMEM((2, slots, 2 * taps, 2 * rows), F32),
+            pltpu.VMEM((2, slots, 2 * taps, 2 * rows), F32),
+            pltpu.VMEM((2 * slots, 2 * block, lanes), F32),
+            pltpu.VMEM((n, rows, lanes), F32),
+            pltpu.VMEM((2 * rows, lanes), F32),
+            pltpu.VMEM((chunks, n, rows, lanes), BF16),
+            pltpu.VMEM((chunks, fou, n, 1, lanes), F32),
+            pltpu.VMEM((chunks, fou * slab, line), BF16),
+            pltpu.VMEM((chunks, fou, n, 1, lanes), F32),
+            pltpu.VMEM((chunks, fou * slab, cols), BF16),
+            pltpu.VMEM((chunks, fou * slab, cols), BF16),
+            dma((chunks,)), dma((chunks,)), dma((chunks, 2)), dma((chunks, 2)),
+            dma((chunks, devices)), dma((chunks, devices)), dma((chunks, devices)), dma((chunks, devices)),
+            dma((chunks, devices)), dma((chunks, devices)), dma((chunks, devices)), dma((chunks, devices)),
+            dma((chunks,)), dma((chunks,)),
+        ],
+        compiler_params=pltpu.CompilerParams(collective_id=0, has_side_effects=True),
+        name="core",
+    )(sky, gram, slot, *consts)
+
+
+def plain_gram(sky, tile_slots, tile_count, gram_tiles):
+    channels, rows, cols = sky.shape
+    fou = lax.axis_size("fou")
+    img = lax.axis_size("img")
+    devices = img * fou
+    line = cols * fou
+    block = gram_tiles.shape[-1]
+    slots = gram_tiles.shape[2]
+    tiles = line // block
+    slab = rows // fou
+    width = line // devices
+    axes = ("img", "fou")
+
+    by_row, cos_turn, sin_turn = tables(line, block)
+    e = jnp.asarray(by_row)
+    et = jnp.asarray(np.ascontiguousarray(by_row.T))
+    es = jnp.concatenate([-et[:, block:], et[:, :block]], axis=1)
+    lanes = 2 * block
+    pc = jnp.broadcast_to(jnp.asarray(cos_turn)[:, :, None], (tiles, tiles, lanes))
+    ps = jnp.broadcast_to(jnp.asarray(sin_turn)[:, :, None], (tiles, tiles, lanes))
+    rc = jnp.tile(jnp.asarray(cos_turn), (1, line // tiles))
+    rs = jnp.tile(jnp.asarray(sin_turn), (1, line // tiles))
+
+    lines = lax.all_to_all(sky.astype(BF16), "fou", split_axis=1, concat_axis=2, tiled=True)
+    spread = forward(lines.reshape(channels * slab, line), et, es, pc, ps)
+    spread = spread.reshape(tiles, channels, slab, lanes)
+    per = block // width
+    if per > 1:
+        spread = spread.reshape(tiles, channels, slab, 2, per, width)
+        spread = spread.transpose(0, 4, 1, 2, 3, 5).reshape(devices, channels, slab, 2 * width)
+    moved = lax.all_to_all(spread, axes, split_axis=0, concat_axis=0, tiled=True)
+
+    which = lax.axis_index("fou") * width // block
+    tile_g = lax.dynamic_index_in_dim(gram_tiles, which, 1, keepdims=False).astype(F32)
+    chosen = lax.dynamic_index_in_dim(tile_slots, which, 1, keepdims=False)
+    used = lax.dynamic_index_in_dim(tile_count, which, 1, keepdims=False)
+    in_use = jnp.arange(slots)[None, :] < used[:, None]
+    tile_g = jnp.where(in_use[:, :, None, None], jnp.swapaxes(tile_g, -1, -2), 0.0)
+
+    if slab % 16:
+        x = moved.transpose(1, 0, 2, 3).reshape(1, channels, line, 2 * width)
+    else:
+        x = moved
+    y = gram(x, chosen, tile_g, e, et, es, rc, rs, pc, ps)
+    if slab % 16:
+        y = y.reshape(channels, devices, slab, 2 * width).transpose(1, 0, 2, 3)
+    back = lax.all_to_all(y, axes, split_axis=0, concat_axis=0, tiled=True)
+    if per > 1:
+        back = back.reshape(tiles, per, channels, slab, 2, width).transpose(0, 2, 3, 4, 1, 5)
+    back = back.reshape(tiles, channels * slab, lanes)
+    final = backward(back, et, es, pc, ps, 1.0 / float(line * line))
+    return lax.all_to_all(
+        final.reshape(channels, slab, line), "fou", split_axis=2, concat_axis=1, tiled=True
+    ).astype(F32)
+
+
+def paired_gram(sky, tile_slots, tile_count, gram_tiles):
+    line = sky.shape[2] * lax.axis_size("fou")
+    slots = tile_slots.shape[2]
+    used = jnp.arange(slots)[None, None, :] < tile_count[:, :, None]
+    slot = jnp.where(used, tile_slots, -1).astype(F32)
+    slot = jnp.pad(slot, ((0, 0), (0, 0), (0, -slots % 8)), constant_values=-1.0)
+    slot = jnp.broadcast_to(slot[..., None], slot.shape + (2 * gram_tiles.shape[-1],))
+    return core(sky, gram_tiles, slot, line, lax.axis_size("img"), lax.axis_size("fou"), gram_tiles.shape[-1])
+
+
+def pairs_up(sky, gram_tiles):
+    img, fou = lax.axis_size("img"), lax.axis_size("fou")
+    channels, rows, cols = sky.shape
+    line, block = cols * fou, gram_tiles.shape[-1]
+    return (fou == 2 and channels % 2 == 0 and 2 * block == LANES and line == 2 * block * img
+            and block % img == 0 and block // img == 4 and rows == LANES)
+
+
 def body(sky, dual, dirty, filters, thresholds, facet_rows, tile_slots, tile_count, gram_tiles):
     channels, rows, cols = sky.shape
     taps_len = filters.shape[1]
@@ -284,25 +896,6 @@
     slab = rows // fou
     width = line // devices
     axes = ("img", "fou")
-
-    by_row, cos_turn, sin_turn = tables(line, block)
-    e = jnp.asarray(by_row)
-    et = jnp.asarray(np.ascontiguousarray(by_row.T))
-    es = jnp.concatenate([-et[:, block:], et[:, :block]], axis=1)
-    lanes = 2 * block
-    pc = jnp.broadcast_to(jnp.asarray(cos_turn)[:, :, None], (tiles, tiles, lanes))
-    ps = jnp.broadcast_to(jnp.asarray(sin_turn)[:, :, None], (tiles, tiles, lanes))
-    rc = jnp.tile(jnp.asarray(cos_turn), (1, line // tiles))
-    rs = jnp.tile(jnp.asarray(sin_turn), (1, line // tiles))
-
-    lines = lax.all_to_all(sky.astype(BF16), "fou", split_axis=1, concat_axis=2, tiled=True)
-    spread = forward(lines.reshape(channels * slab, line), et, es, pc, ps)
-    spread = spread.reshape(tiles, channels, slab, lanes)
-    per = block // width
-    if per > 1:
-        spread = spread.reshape(tiles, channels, slab, 2, per, width)
-        spread = spread.transpose(0, 4, 1, 2, 3, 5).reshape(devices, channels, slab, 2 * width)
-    moved = lax.all_to_all(spread, axes, split_axis=0, concat_axis=0, tiled=True)
 
     identity = (jnp.arange(taps_len) == radius).astype(F32)
     taps = jnp.concatenate([identity[None], filters], axis=0)
@@ -331,28 +924,8 @@
         + jnp.pad(from_below, ((0, 0), (rest, 0), (0, 0)))
     )
 
-    which = lax.axis_index("fou") * width // block
-    tile_g = lax.dynamic_index_in_dim(gram_tiles, which, 1, keepdims=False).astype(F32)
-    chosen = lax.dynamic_index_in_dim(tile_slots, which, 1, keepdims=False)
-    used = lax.dynamic_index_in_dim(tile_count, which, 1, keepdims=False)
-    in_use = jnp.arange(slots)[None, :] < used[:, None]
-    tile_g = jnp.where(in_use[:, :, None, None], jnp.swapaxes(tile_g, -1, -2), 0.0)
-
-    if slab % 16:
-        x = moved.transpose(1, 0, 2, 3).reshape(1, channels, line, 2 * width)
-    else:
-        x = moved
-    y = gram(x, chosen, tile_g, e, et, es, rc, rs, pc, ps)
-    if slab % 16:
-        y = y.reshape(channels, devices, slab, 2 * width).transpose(1, 0, 2, 3)
-    back = lax.all_to_all(y, axes, split_axis=0, concat_axis=0, tiled=True)
-    if per > 1:
-        back = back.reshape(tiles, per, channels, slab, 2, width).transpose(0, 2, 3, 4, 1, 5)
-    back = back.reshape(tiles, channels * slab, lanes)
-    final = backward(back, et, es, pc, ps, 1.0 / float(line * line))
-    gram_image = lax.all_to_all(
-        final.reshape(channels, slab, line), "fou", split_axis=2, concat_axis=1, tiled=True
-    ).astype(F32)
+    find = paired_gram if pairs_up(sky, gram_tiles) else plain_gram
+    gram_image = find(sky, tile_slots, tile_count, gram_tiles)
 
     live_rows = (jnp.arange(rows, dtype=jnp.int32) < facet_rows[0]).astype(F32)
     image_next = (

time: 272 us -> 210 us (0.77)
  Pallas kernels: 81.2 us -> 147 us
  waiting for transfers between devices: 60.9 us -> 9.26 us
  local copies, waits for them, and re-layouts: 52.7 us -> 8.71 us
  blocking collectives: 17.7 us -> 0 us
  starting transfers between devices: 32.8 us -> 18 us
    pallas_call x3 -> x1, Pallas kernels: 49.2 us -> 115 us  [core(): pl.pallas_call(functools.partial(core_kernel, 1.0 / float(line * line)),...]
    all_to_all x3 -> x0, waiting for transfers between devices: 60.9 us -> none  [the longest x1 39.7 us: body(): lax.all_to_all(spread, axes, split_axis=0, concat_axis=0, tiled=True)]
    unnamed x266 -> x120, local copies, waits for them, and re-layouts: 23.5 us -> 0.72 us
    all_to_all x1 -> x0, blocking collectives: 17.7 us -> none  [body(): lax.all_to_all(sky.astype(BF16), 'fou', split_axis=1, concat_axis=2, tile...]
    all_to_all x3 -> x0, starting transfers between devices: 12.5 us -> none  [the longest x1 5.05 us: body(): lax.all_to_all(spread, axes, split_axis=0, concat_axis=0, tiled=True)]
    another operation x4 -> x0, local copies, waits for them, and re-layouts: 6.98 us -> none  [the longest x2 3.5 us: body(): rc = jnp.tile(jnp.asarray(cos_turn), (1, line // tiles))]
    convert_element_type x2 -> x0, local copies, waits for them, and re-layouts: 5.45 us -> none  [body(): gram_image = lax.all_to_all(final.reshape(channels, slab, line), 'fou', s...]
    ppermute x4, waiting for transfers between devices: 0.01 us -> 5.12 us  [shift_up(): return lax.ppermute(x, axis, [(i, i + 1) for i in range(count - 1)])]
  transfers between devices with their start and end apart: 11 -> 8, of which waited for: 2 -> 3; matrix products, arithmetic and copies ran while one was open for 21% -> 3% of each run, Pallas kernels for 9% -> 55%
where the time goes in v1:
time: 210 us; the launch traced here: 208 us
  Pallas kernels  147 us (70%)
  other arithmetic  22.6 us (11%)
  starting transfers between devices  18 us (9%)
  waiting for transfers between devices  9.26 us (4%)
  local copies, waits for them, and re-layouts  8.71 us (4%)
  between operations  2.38 us (1%)
    pallas_call x1, Pallas kernels, core(): pl.pallas_call(functools.partial(core_kernel, 1.0 / float(line * line)),...  115 us
    pallas_call x1, Pallas kernels, analyse(): pl.pallas_call(analysis_kernel, grid=(frames,), in_specs=[pl.BlockSpec(me...  20.9 us
    ppermute x4, starting transfers between devices, shift_up(): return lax.ppermute(x, axis, [(i, i + 1) for i in range(count - 1)])  12.7 us
    convert_element_type x4, other arithmetic, banded(): return out.astype(BF16)  11.9 us
    pallas_call x1, Pallas kernels, synthesize(): pl.pallas_call(synthesis_kernel, grid=(channels,), in_specs=[pl.BlockSpec...  11.1 us
    convert_element_type x1, other arithmetic, body(): probe = (2.0 * image_next - sky).astype(BF16)  5.38 us
    ppermute x4, starting transfers between devices, shift_down(): return lax.ppermute(x, axis, [(i + 1, i) for i in range(count - 1)])  5.35 us
    ppermute x4, waiting for transfers between devices, shift_up(): return lax.ppermute(x, axis, [(i, i + 1) for i in range(count - 1)])  5.12 us
  transfers between devices with their start and end apart: 8, of which 3 were waited for; matrix products, arithmetic and copies ran while one was open for 3% of the time, Pallas kernels for 55%

profile of v1, /device:TPU:0, one launch (start us, length us, event | category | flops | bytes accessed | tf_op | source)
XLA Modules:
  0.0 208.0 jit_solution(17244152130297285387)
XLA Ops:
  0.7 1.3 fusion.28
  2.0 1.4 fusion.10
  4.1 3.8 %select_convert_fusion.2.col_ref = bf16[9,256,128]{2,1,0:T(8,128)(2,1)} fusion(bf16[9]{0:T(256)(128)(2,1)S(1)} %get-tuple-element.17, bf16[9]{0:T(256)(128)(2,1)S(1)} %get-tuple-element.18, bf16[9]{0:T(256)(128)(2,1)S(1)} %get-tuple-element.16, bf16[9]{0:T(256)(128)(2,1)S(1)} %get-tuple-element.15, bf16[9]{0:T(256)(128)(2,1)S(1)} %get-tuple-element.14, ...), kind=kLoop, calls=%fused_computation.13 | loop fusion | flops 5013504 | bytes 1147186 | tf_op jit(solution)/shard_map/convert_element_type | solution.py:260
  7.9 0.8 broadcast_in_dim.944
  8.7 0.8 broadcast_in_dim.949
  9.7 0.1 broadcast_in_dim.959
  9.9 0.1 broadcast_in_dim.969
  11.0 2.3 %select_convert_fusion.3.row_ref = bf16[144,1152]{1,0:T(8,128)(2,1)} fusion(pred[18,8,9,128]{3,2,1,0:T(8,128)(4,1)S(1)} %bitcast.137, pred[18,8,9,128]{3,2,1,0:T(8,128)(4,1)S(1)} %bitcast.136, pred[18,8,9,128]{3,2,1,0:T(8,128)(4,1)S(1)} %bitcast.135, pred[18,8,9,128]{3,2,1,0:T(8,128)(4,1)S(1)} %bitcast.134, pred[18,8,9,128]{3,2,1,0:T(8,128)(4,1)S(1)} %bitcast.133, ...), kind=kLoop, calls=%fused_computation.14 | loop fusion | flops 2820096 | bytes 3191040 | tf_op jit(solution)/shard_map/convert_element_type | solution.py:260
  13.3 11.1 %synthesis.1 = f32[4,144,1152]{2,1,0:T(8,128)} custom-call(bf16[4,9,128,1024]{3,2,1,0:T(8,128)(2,1)} %d_ref.3, bf16[9,256,128]{2,1,0:T(8,128)(2,1)} %select_convert_fusion.2.col_ref, bf16[144,1152]{1,0:T(8,128)(2,1)} %select_convert_fusion.3.row_ref), custom_call_target="tpu_custom_call" | custom-call | flops 4246732800 | bytes 9437184 | tf_op jit(solution)/shard_map/synthesis/pallas_call | solution.py:198
  24.4 1.2 fusion.42
  25.6 4.9 %collective-permute-start = (f32[4,144,8]{2,1,0:T(8,128)S(1)}, f32[4,144,8]{2,1,0:T(8,128)S(1)}, u32[]{:S(2)}, u32[]{:S(2)}) collective-permute-start(f32[4,144,8]{2,1,0:T(8,128)S(1)} %get-tuple-element.21), channel_id=1, source_target_pairs={{0,1},{2,3},{4,5},{6,7},{8,9},{10,11},{12,13},{14,15},{16,17},{18,... | collective-permute-start | bytes 55304 | tf_op jit(solution)/shard_map/ppermute | solution.py:265
  30.6 1.3 collective-permute-start.1
  31.9 0.1 copy.31
  32.1 4.6 %collective-permute-done = f32[4,144,8]{2,1,0:T(8,128)S(1)} collective-permute-done((f32[4,144,8]{2,1,0:T(8,128)S(1)}, f32[4,144,8]{2,1,0:T(8,128)S(1)}, u32[]{:S(2)}, u32[]{:S(2)}) %collective-permute-start) | collective-permute-done | bytes 18464 | tf_op jit(solution)/shard_map/ppermute | solution.py:265
  36.8 4.1 %collective-permute-done.1 = f32[4,144,8]{2,1,0:T(8,128)S(1)} collective-permute-done((f32[4,144,8]{2,1,0:T(8,128)S(1)}, f32[4,144,8]{2,1,0:T(8,128)S(1)}, u32[]{:S(2)}, u32[]{:S(2)}) %collective-permute-start.1) | collective-permute-done | bytes 18464 | tf_op jit(solution)/shard_map/ppermute | solution.py:270
  40.9 2.5 %fusion = f32[4,144,1024]{2,1,0:T(8,128)S(1)} fusion(f32[4,144,1152]{2,1,0:T(8,128)} %synthesis.1, f32[4,144,8]{2,1,0:T(8,128)S(1)} %collective-permute-done.1, f32[4,144,8]{2,1,0:T(8,128)S(1)} %collective-permute-done), kind=kLoop, calls=%fused_computation.1 | loop fusion | flops 1179648 | bytes 4755456 | tf_op jit(solution)/shard_map/add | solution.py:915
  43.4 1.3 collective-permute-start.2
  44.7 1.5 collective-permute-start.3
  47.5 0.7 broadcast_in_dim.892.slot
  48.2 115.0 %core.1 = f32[4,128,1024]{2,1,0:T(8,128)} custom-call(f32[4,128,1024]{2,1,0:T(8,128)} %sky.1, bf16[4,2,6,64,64]{4,3,2,1,0:T(8,128)(2,1)} %gram.1, f32[4,2,8,128]{3,2,1,0:T(8,128)} %broadcast_in_dim.892.slot, f32[2048,128]{1,0:T(8,128)} %constant.69.clone.base, f32[16,16,128]{2,1,0:T(8,128)} %constant.70.clone.turn_c, f32[16,16,128]{2,1,0:T(8,128)} %constant.71.clone.turn_s, ...), custom_call_target="tpu_custom_call" | custom-call | tf_op jit(solution)/shard_map/core/pallas_call | solution.py:772
  163.3 5.4 %subtract_convert_fusion = (bf16[4,128,1024]{2,1,0:T(8,128)(2,1)S(1)}, f32[4,128,1024]{2,1,0:T(8,128)}) fusion(f32[4,128,1024]{2,1,0:T(8,128)} %sky.1, f32[128]{0:T(128)S(1)} %compare_convert_fusion, f32[4,8,1024]{2,1,0:T(8,128)S(1)} %collective-permute-done.3, f32[4,8,1024]{2,1,0:T(8,128)S(1)} %collective-permute-done.2, f32[4,144,1024]{2,1,0:T(8,128)S(1)} %fusion, ...), kind=kLoop, calls=%fused_computation.9 | loop fusion | flops 5767168 | bytes 11796992 | tf_op jit(solution)/shard_map/convert_element_type | solution.py:935
  168.9 1.7 collective-permute-start.4
  170.6 1.3 collective-permute-start.5
  171.9 2.9 %select_convert_fusion.row_ref = bf16[9,128,144]{2,1,0:T(8,128)(2,1)} fusion(bf16[9]{0:T(256)(128)(2,1)S(1)} %get-tuple-element.17, bf16[9]{0:T(256)(128)(2,1)S(1)} %get-tuple-element.18, bf16[9]{0:T(256)(128)(2,1)S(1)} %get-tuple-element.16, bf16[9]{0:T(256)(128)(2,1)S(1)} %get-tuple-element.15, bf16[9]{0:T(256)(128)(2,1)S(1)} %get-tuple-element.14, ...), kind=kLoop, calls=%fused_computation.11 | loop fusion | flops 2820096 | bytes 645426 | tf_op jit(solution)/shard_map/convert_element_type | solution.py:260
  174.8 0.1 pad_maximum_fusion
  174.9 0.1 fusion.44
  175.0 1.3 collective-permute-start.7
  176.3 4.8 %collective-permute-start.6 = (bf16[4,144,8]{2,1,0:T(8,128)(2,1)S(1)}, bf16[4,144,8]{2,1,0:T(8,128)(2,1)S(1)}, u32[]{:S(2)}, u32[]{:S(2)}) collective-permute-start(bf16[4,144,8]{2,1,0:T(8,128)(2,1)S(1)} %get-tuple-element.26), channel_id=1, source_target_pairs={{0,1},{2,3},{4,5},{6,7},{8,9},{10,11},{12,13},{14,15},{16,17},{18,... | collective-permute-start | bytes 27656 | tf_op jit(solution)/shard_map/ppermute | solution.py:265
  181.2 2.9 %select_convert_fusion.1.col_ref = bf16[9,256,128]{2,1,0:T(8,128)(2,1)} fusion(bf16[9]{0:T(256)(128)(2,1)S(1)} %get-tuple-element.17, bf16[9]{0:T(256)(128)(2,1)S(1)} %get-tuple-element.18, bf16[9]{0:T(256)(128)(2,1)S(1)} %get-tuple-element.16, bf16[9]{0:T(256)(128)(2,1)S(1)} %get-tuple-element.15, bf16[9]{0:T(256)(128)(2,1)S(1)} %get-tuple-element.14, ...), kind=kLoop, calls=%fused_computation.12 | loop fusion | flops 5013504 | bytes 1147186 | tf_op jit(solution)/shard_map/convert_element_type | solution.py:260
  184.2 0.5 collective-permute-done.6
  184.7 2.4 %concatenate.11.p_ref = bf16[4,144,1152]{2,1,0:T(8,128)(2,1)} concatenate(bf16[4,144,8]{2,1,0:T(8,128)(2,1)S(1)} %collective-permute-done.6, bf16[4,144,1024]{2,1,0:T(8,128)(2,1)S(1)} %pad_maximum_fusion, bf16[4,144,8]{2,1,0:T(8,128)(2,1)S(1)} %collective-permute-done.7, bf16[4,144,112]{2,1,0:T(8,128)(2,1)S(1)} %broadcast_in_dim.1030), dimensions={2} | concatenate | bytes 2654208 | tf_op jit(solution)/shard_map/concatenate | solution.py:940
  187.1 20.9 %analysis.1 = bf16[4,9,128,1024]{3,2,1,0:T(8,128)(2,1)} custom-call(f32[9]{0:T(128)} %bound_ref.1, bf16[4,144,1152]{2,1,0:T(8,128)(2,1)} %concatenate.11.p_ref, bf16[4,9,128,1024]{3,2,1,0:T(8,128)(2,1)} %d_ref.3, bf16[9,256,128]{2,1,0:T(8,128)(2,1)} %select_convert_fusion.1.col_ref, bf16[9,128,144]{2,1,0:T(8,128)(2,1)} %select_convert_fusion.row_ref), custom_call_target="tpu_custom_call" | custom-call | tf_op jit(solution)/shard_map/analysis/pallas_call | solution.py:237
  (153 shorter events, 2.5 us)
Async XLA Ops:
  13.3 18.5 %copy-start.50 = (s32[4,2]{0,1:T(2,128)S(1)}, s32[4,2]{0,1:T(2,128)}, u32[]{:S(2)}) copy-start(s32[4,2]{0,1:T(2,128)} %param.35) | copy-start | bytes 100
  25.6 11.2 %collective-permute-start = (f32[4,144,8]{2,1,0:T(8,128)S(1)}, f32[4,144,8]{2,1,0:T(8,128)S(1)}, u32[]{:S(2)}, u32[]{:S(2)}) collective-permute-start(f32[4,144,8]{2,1,0:T(8,128)S(1)} %get-tuple-element.21), channel_id=1, source_target_pairs={{0,1},{2,3},{4,5},{6,7},{8,9},{10,11},{12,13},{14,15},{16,17},{18,... | collective-permute-start | bytes 55304 | tf_op jit(solution)/shard_map/ppermute | solution.py:265
  30.6 10.4 %collective-permute-start.1 = (f32[4,144,8]{2,1,0:T(8,128)S(1)}, f32[4,144,8]{2,1,0:T(8,128)S(1)}, u32[]{:S(2)}, u32[]{:S(2)}) collective-permute-start(f32[4,144,8]{2,1,0:T(8,128)S(1)} %get-tuple-element.22), channel_id=1, source_target_pairs={{1,0},{3,2},{5,4},{7,6},{9,8},{11,10},{13,12},{15,14},{17,16},{19,... | collective-permute-start | bytes 55304 | tf_op jit(solution)/shard_map/ppermute | solution.py:270
  32.0 14.3 %copy-start.49 = (s32[4,2,6]{2,1,0:T(2,128)S(1)}, s32[4,2,6]{2,1,0:T(2,128)}, u32[]{:S(2)}) copy-start(s32[4,2,6]{2,1,0:T(2,128)} %param.34) | copy-start | bytes 580
  32.0 15.0 %copy-start.33 = (pred[128,144]{1,0:T(32,128)(4,1)S(1)}, pred[128,144]{1,0:T(32,128)(4,1)}, u32[]{:S(2)}) copy-start(pred[128,144]{1,0:T(32,128)(4,1)} %constant.208) | copy-start | bytes 55300
  32.0 15.0 %copy-start.32 = (pred[128,144]{1,0:T(32,128)(4,1)S(1)}, pred[128,144]{1,0:T(32,128)(4,1)}, u32[]{:S(2)}) copy-start(pred[128,144]{1,0:T(32,128)(4,1)} %constant.209) | copy-start | bytes 55300
  32.0 15.1 %copy-start.31 = (pred[128,144]{1,0:T(32,128)(4,1)S(1)}, pred[128,144]{1,0:T(32,128)(4,1)}, u32[]{:S(2)}) copy-start(pred[128,144]{1,0:T(32,128)(4,1)} %constant.210) | copy-start | bytes 55300
  32.0 15.1 %copy-start.30 = (pred[128,144]{1,0:T(32,128)(4,1)S(1)}, pred[128,144]{1,0:T(32,128)(4,1)}, u32[]{:S(2)}) copy-start(pred[128,144]{1,0:T(32,128)(4,1)} %constant.211) | copy-start | bytes 55300
  32.0 15.1 %copy-start.29 = (pred[128,144]{1,0:T(32,128)(4,1)S(1)}, pred[128,144]{1,0:T(32,128)(4,1)}, u32[]{:S(2)}) copy-start(pred[128,144]{1,0:T(32,128)(4,1)} %constant.212) | copy-start | bytes 55300
  32.0 15.1 %copy-start.28 = (pred[128,144]{1,0:T(32,128)(4,1)S(1)}, pred[128,144]{1,0:T(32,128)(4,1)}, u32[]{:S(2)}) copy-start(pred[128,144]{1,0:T(32,128)(4,1)} %constant.213) | copy-start | bytes 55300
  32.0 15.2 %copy-start.27 = (pred[128,144]{1,0:T(32,128)(4,1)S(1)}, pred[128,144]{1,0:T(32,128)(4,1)}, u32[]{:S(2)}) copy-start(pred[128,144]{1,0:T(32,128)(4,1)} %constant.214) | copy-start | bytes 55300
  32.0 15.2 %copy-start.26 = (pred[128,144]{1,0:T(32,128)(4,1)S(1)}, pred[128,144]{1,0:T(32,128)(4,1)}, u32[]{:S(2)}) copy-start(pred[128,144]{1,0:T(32,128)(4,1)} %constant.215) | copy-start | bytes 55300
  32.0 15.2 %copy-start.25 = (pred[128,144]{1,0:T(32,128)(4,1)S(1)}, pred[128,144]{1,0:T(32,128)(4,1)}, u32[]{:S(2)}) copy-start(pred[128,144]{1,0:T(32,128)(4,1)} %constant.216) | copy-start | bytes 55300
  32.0 15.2 %copy-start.24 = (pred[128,144]{1,0:T(32,128)(4,1)S(1)}, pred[128,144]{1,0:T(32,128)(4,1)}, u32[]{:S(2)}) copy-start(pred[128,144]{1,0:T(32,128)(4,1)} %constant.217) | copy-start | bytes 55300
  32.1 15.2 %copy-start.23 = (pred[128,144]{1,0:T(32,128)(4,1)S(1)}, pred[128,144]{1,0:T(32,128)(4,1)}, u32[]{:S(2)}) copy-start(pred[128,144]{1,0:T(32,128)(4,1)} %constant.218) | copy-start | bytes 55300
  32.1 15.3 %copy-start.22 = (pred[128,144]{1,0:T(32,128)(4,1)S(1)}, pred[128,144]{1,0:T(32,128)(4,1)}, u32[]{:S(2)}) copy-start(pred[128,144]{1,0:T(32,128)(4,1)} %constant.219) | copy-start | bytes 55300
  32.1 15.3 %copy-start.21 = (pred[128,144]{1,0:T(32,128)(4,1)S(1)}, pred[128,144]{1,0:T(32,128)(4,1)}, u32[]{:S(2)}) copy-start(pred[128,144]{1,0:T(32,128)(4,1)} %constant.220) | copy-start | bytes 55300
  32.1 15.3 %copy-start.20 = (pred[128,144]{1,0:T(32,128)(4,1)S(1)}, pred[128,144]{1,0:T(32,128)(4,1)}, u32[]{:S(2)}) copy-start(pred[128,144]{1,0:T(32,128)(4,1)} %constant.221) | copy-start | bytes 55300
  32.1 15.3 %copy-start.19 = (pred[128,144]{1,0:T(32,128)(4,1)S(1)}, pred[128,144]{1,0:T(32,128)(4,1)}, u32[]{:S(2)}) copy-start(pred[128,144]{1,0:T(32,128)(4,1)} %constant.222) | copy-start | bytes 55300
  32.1 15.3 %copy-start.18 = (pred[128,144]{1,0:T(32,128)(4,1)S(1)}, pred[128,144]{1,0:T(32,128)(4,1)}, u32[]{:S(2)}) copy-start(pred[128,144]{1,0:T(32,128)(4,1)} %constant.223) | copy-start | bytes 55300
  32.1 15.4 %copy-start.17 = (pred[128,144]{1,0:T(32,128)(4,1)S(1)}, pred[128,144]{1,0:T(32,128)(4,1)}, u32[]{:S(2)}) copy-start(pred[128,144]{1,0:T(32,128)(4,1)} %constant.224) | copy-start | bytes 55300
  43.4 119.8 %collective-permute-start.2 = (f32[4,8,1024]{2,1,0:T(8,128)S(1)}, f32[4,8,1024]{2,1,0:T(8,128)S(1)}, u32[]{:S(2)}, u32[]{:S(2)}) collective-permute-start(f32[4,8,1024]{2,1,0:T(8,128)S(1)} %get-tuple-element.23), channel_id=1, source_target_pairs={{0,2},{2,4},{4,6},{6,8},{8,10},{10,12},{12,14},{14,16},{16,18},{18... | collective-permute-start | bytes 393224 | tf_op jit(solution)/shard_map/ppermute | solution.py:265
  44.7 118.6 %collective-permute-start.3 = (f32[4,8,1024]{2,1,0:T(8,128)S(1)}, f32[4,8,1024]{2,1,0:T(8,128)S(1)}, u32[]{:S(2)}, u32[]{:S(2)}) collective-permute-start(f32[4,8,1024]{2,1,0:T(8,128)S(1)} %get-tuple-element.24), channel_id=1, source_target_pairs={{2,0},{4,2},{6,4},{8,6},{10,8},{12,10},{14,12},{16,14},{18,16},{20... | collective-permute-start | bytes 393224 | tf_op jit(solution)/shard_map/ppermute | solution.py:270
  168.7 12.4 %copy-start = (pred[256,128]{1,0:T(32,128)(4,1)S(1)}, pred[256,128]{1,0:T(32,128)(4,1)}, u32[]{:S(2)}) copy-start(pred[256,128]{1,0:T(32,128)(4,1)} %constant.207) | copy-start | bytes 98308
  168.7 12.4 %copy-start.1 = (pred[256,128]{1,0:T(32,128)(4,1)S(1)}, pred[256,128]{1,0:T(32,128)(4,1)}, u32[]{:S(2)}) copy-start(pred[256,128]{1,0:T(32,128)(4,1)} %constant.206) | copy-start | bytes 98308
  168.7 12.4 %copy-start.2 = (pred[256,128]{1,0:T(32,128)(4,1)S(1)}, pred[256,128]{1,0:T(32,128)(4,1)}, u32[]{:S(2)}) copy-start(pred[256,128]{1,0:T(32,128)(4,1)} %constant.205) | copy-start | bytes 98308
  168.7 12.4 %copy-start.3 = (pred[256,128]{1,0:T(32,128)(4,1)S(1)}, pred[256,128]{1,0:T(32,128)(4,1)}, u32[]{:S(2)}) copy-start(pred[256,128]{1,0:T(32,128)(4,1)} %constant.204) | copy-start | bytes 98308
  168.8 12.4 %copy-start.4 = (pred[256,128]{1,0:T(32,128)(4,1)S(1)}, pred[256,128]{1,0:T(32,128)(4,1)}, u32[]{:S(2)}) copy-start(pred[256,128]{1,0:T(32,128)(4,1)} %constant.203) | copy-start | bytes 98308
  168.9 5.9 %collective-permute-start.4 = (bf16[4,8,1024]{2,1,0:T(8,128)(2,1)S(1)}, bf16[4,8,1024]{2,1,0:T(8,128)(2,1)S(1)}, u32[]{:S(2)}, u32[]{:S(2)}) collective-permute-start(bf16[4,8,1024]{2,1,0:T(8,128)(2,1)S(1)} %get-tuple-element.27), channel_id=1, source_target_pairs={{0,2},{2,4},{4,6},{6,8},{8,10},{10,12},{12,14},{14,16},{16,18},{18... | collective-permute-start | bytes 196616 | tf_op jit(solution)/shard_map/ppermute | solution.py:265
  170.6 4.2 %collective-permute-start.5 = (bf16[4,8,1024]{2,1,0:T(8,128)(2,1)S(1)}, bf16[4,8,1024]{2,1,0:T(8,128)(2,1)S(1)}, u32[]{:S(2)}, u32[]{:S(2)}) collective-permute-start(bf16[4,8,1024]{2,1,0:T(8,128)(2,1)S(1)} %get-tuple-element.28), channel_id=1, source_target_pairs={{2,0},{4,2},{6,4},{8,6},{10,8},{12,10},{14,12},{16,14},{18,16},{20... | collective-permute-start | bytes 196616 | tf_op jit(solution)/shard_map/ppermute | solution.py:270
  175.0 9.2 %collective-permute-start.7 = (bf16[4,144,8]{2,1,0:T(8,128)(2,1)S(1)}, bf16[4,144,8]{2,1,0:T(8,128)(2,1)S(1)}, u32[]{:S(2)}, u32[]{:S(2)}) collective-permute-start(bf16[4,144,8]{2,1,0:T(8,128)(2,1)S(1)} %get-tuple-element.25), channel_id=1, source_target_pairs={{1,0},{3,2},{5,4},{7,6},{9,8},{11,10},{13,12},{15,14},{17,16},{19,... | collective-permute-start | bytes 27656 | tf_op jit(solution)/shard_map/ppermute | solution.py:270
  176.3 8.3 %collective-permute-start.6 = (bf16[4,144,8]{2,1,0:T(8,128)(2,1)S(1)}, bf16[4,144,8]{2,1,0:T(8,128)(2,1)S(1)}, u32[]{:S(2)}, u32[]{:S(2)}) collective-permute-start(bf16[4,144,8]{2,1,0:T(8,128)(2,1)S(1)} %get-tuple-element.26), channel_id=1, source_target_pairs={{0,1},{2,3},{4,5},{6,7},{8,9},{10,11},{12,13},{14,15},{16,17},{18,... | collective-permute-start | bytes 27656 | tf_op jit(solution)/shard_map/ppermute | solution.py:265
  (27 other events, 244.9 us)
